TPU v7x, 128 devices: a whole 4x4x4 slice. The times are simulated.
128 devices in a mesh: band: 4 (over y), dom: 32 (over x, z, core).
Axes of the slice: x: 4, y: 4, z: 4, core: 2. Of those that a mesh axis runs over, the one named last changes fastest.
Arguments:
- orbitals: float32 [1024, 131072], P('band', 'dom'), may hold values from -6 to 6
- projectors: float32 [1024, 512, 128], P('dom'), may hold values from -0.25 to 0.25
- window_start: int32 [1024], P('dom'), may hold values from 0 to 3584
- slot_atom: int32 [32, 32], replicated, may hold values from 0 to 95, as said below
- atom_home: int32 [96], replicated, may hold values from 0 to 95, as said below
- atom_matrices: float32 [96, 128, 128], P('dom'), may hold values from -0.1875 to 0.1875
- rotation: float32 [1024, 1024], P('band'), may hold values from -0.1875 to 0.1875
Outputs:
- rotated: float32 [1024, 131072], P('band', 'dom')
Inputs may be any that keep to these rules, and one draw needn't show every extreme that they name: `atom_home`: a permutation; atom a is owned by domain atom_home[a] // 3, so every domain owns 3 atoms. `slot_atom`: in one domain at most 2 windows have atoms of one owner; in every domain some owner has exactly 2 of them, and some owner has exactly 2 from every domain.
All inputs are finite; a program needn't handle non-finite values.
Results may differ from a plain program's by a relative error of at most 0.0003.
Values sent between devices are 32-bit elements; how exact they have to be, the bound alone decides.
A program may use at most 128 MiB of HBM per device.

v0:
```python
import jax
import jax.numpy as jnp
from jax import lax
from jax.sharding import PartitionSpec as P

HIGHEST = lax.Precision.HIGHEST


def per_device(orbitals, projectors, window_start, slot_atom, atom_home, atom_matrices, rotation):
    own_domain = lax.axis_index("dom")
    slot_count = projectors.shape[0]
    window = projectors.shape[1]
    atom_count = atom_home.shape[0]
    windows = jax.vmap(lambda offset: lax.dynamic_slice_in_dim(orbitals, offset, window, 1))(
        window_start
    )
    partials = jnp.einsum("sbw,swp->sbp", windows, projectors, precision=HIGHEST)
    atom_ids = jnp.arange(atom_count, dtype=jnp.int32)
    home_table = jnp.sum(
        jnp.where(slot_atom[:, :, None] == atom_ids[None, None, :], atom_home[None, None, :], 0),
        axis=2,
    )
    own_home = lax.dynamic_index_in_dim(home_table, own_domain, 0, keepdims=False)
    home_match = (atom_ids[:, None] == own_home[None, :]).astype(jnp.float32)
    per_atom = jnp.einsum("rs,sbp->rbp", home_match, partials, precision=HIGHEST)
    owned_sums = lax.psum_scatter(per_atom, "dom", scatter_dimension=0, tiled=True)
    owned_factors = jnp.einsum("abp,apq->abq", owned_sums, atom_matrices, precision=HIGHEST)
    all_factors = lax.all_gather(owned_factors, "dom", axis=0, tiled=True)
    slot_factors = jnp.einsum("rs,rbp->sbp", home_match, all_factors, precision=HIGHEST)
    updates = jnp.einsum("sbq,swq->sbw", slot_factors, projectors, precision=HIGHEST)

    def add_window(slot_index, current):
        offset = window_start[slot_index]
        previous = lax.dynamic_slice_in_dim(current, offset, window, 1)
        return lax.dynamic_update_slice_in_dim(current, previous + updates[slot_index], offset, 1)

    corrected = lax.fori_loop(0, slot_count, add_window, orbitals)
    return jnp.dot(
        rotation,
        lax.all_gather(corrected, "band", axis=0, tiled=True),
        precision=HIGHEST,
        preferred_element_type=jnp.float32,
    )


def solution(mesh):
    in_specs = (
        P("band", "dom"),
        P("dom", None, None),
        P("dom"),
        P(),
        P(),
        P("dom", None, None),
        P("band", None),
    )
    out_specs = P("band", "dom")
    return jax.shard_map(
        per_device, mesh=mesh, in_specs=in_specs, out_specs=out_specs, check_vma=False
    )
```

profile of v0, /device:TPU:1, one launch (start us, length us, event | category | flops | bytes accessed | tf_op | source)
XLA Modules:
  0.0 820.0 jit_solution(12491529230231990169)
XLA Ops:
  6.6 4.7 copy.41
  11.3 107.9 %while.15 = (s32[]{:T(128)}, f32[256,4096]{1,0:T(8,128)}, s32[32,2]{0,1:T(2,128)S(1)}, f32[32,256,512]{2,1,0:T(8,128)}, s32[]{:T(128)}) while((s32[]{:T(128)}, f32[256,4096]{1,0:T(8,128)}, s32[32,2]{0,1:T(2,128)S(1)}, f32[32,256,512]{2,1,0:T(8,128)}, s32[]{:T(128)}) %tuple.39), condition=%wide.while_cond, body=%wide.while_body.sunk | while | flops 2 | bytes 1049689 | solution.py:14
  62.5 2.8 bitcast_dynamic-update-slice_fusion.2
  65.9 2.8 bitcast_dynamic-update-slice_fusion.2
  69.3 2.8 bitcast_dynamic-update-slice_fusion.2
  120.1 19.3 %fusion.12 = f32[32,256,128]{2,1,0:T(8,128)S(1)} fusion(f32[32,256,512]{2,1,0:T(8,128)} %get-tuple-element.92, f32[32,512,128]{2,1,0:T(8,128)} %param.10), kind=kOutput, calls=%fused_computation.19 | convolution fusion | flops 6442450944 | bytes 29360128 | tf_op jit(solution)/shard_map/sbw,swp->sbp/dot_general | solution.py:17
  139.3 11.5 %fusion.4 = f32[96,256,128]{2,0,1:T(8,128)} fusion(f32[32,256,128]{2,1,0:T(8,128)S(1)} %fusion.12, s32[32]{0:T(128)S(1)} %dynamic-slice_bitcast_fusion), kind=kOutput, calls=%fused_computation.8 | convolution fusion | flops 1207962624 | bytes 16777344 | tf_op jit(solution)/shard_map/rs,sbp->rbp/dot_general | solution.py:25
  150.8 16.4 %copy.16 = f32[96,256,128]{2,1,0:T(8,128)} copy(f32[96,256,128]{2,0,1:T(8,128)} %fusion.4) | data formatting | bytes 25165824 | tf_op jit(solution)/shard_map/rs,sbp->rbp/dot_general | solution.py:25
  167.2 106.7 %reduce-scatter.2.cloned.1.call-done = f32[3,256,128]{2,1,0:T(8,128)} async-done(((f32[96,256,128]{2,1,0:T(8,128)}), f32[3,256,128]{2,1,0:T(8,128)}) %reduce-scatter.2.cloned.1.call-update) | async-done | bytes 393232 | tf_op jit(solution)/shard_map/reduce_scatter | solution.py:26
  276.2 63.9 %all-gather.3.cloned.1.call-done = f32[96,256,128]{2,1,0:T(8,128)} async-done(((f32[3,256,128]{2,1,0:T(8,128)}), f32[96,256,128]{2,1,0:T(8,128)}) %all-gather.3.cloned.1.call-update) | async-done | bytes 12582928 | tf_op jit(solution)/shard_map/all_gather | solution.py:28
  340.1 16.1 %fusion = f32[32,256,128]{2,0,1:T(8,128)S(1)} fusion(f32[96,256,128]{2,1,0:T(8,128)} %all-gather.3.cloned.1.call-done, s32[32]{0:T(128)S(1)} %dynamic-slice_bitcast_fusion), kind=kOutput, calls=%fused_computation.3 | convolution fusion | flops 1207962624 | bytes 16777344 | tf_op jit(solution)/shard_map/rs,rbp->sbp/dot_general | solution.py:29
  356.3 20.9 %fusion.2 = f32[32,256,512]{2,1,0:T(8,128)} fusion(f32[32,512,128]{2,1,0:T(8,128)} %param.10, f32[32,256,128]{2,0,1:T(8,128)S(1)} %fusion), kind=kOutput, calls=%fused_computation.6 | convolution fusion | flops 6442450944 | bytes 29360128 | tf_op jit(solution)/shard_map/sbq,swq->sbw/dot_general | solution.py:30
  377.2 247.2 %while.14 = (s32[]{:T(128)}, f32[256,4096]{1,0:T(8,128)}, s32[32]{0:T(128)S(1)}, f32[32,256,512]{2,1,0:T(8,128)}, s32[]{:T(128)}, /*index=5*/s32[]{:T(128)}, s32[]{:T(128)}) while((s32[]{:T(128)}, f32[256,4096]{1,0:T(8,128)}, s32[32]{0:T(128)S(1)}, f32[32,256,512]{2,1,0:T(8,128)}, s32[]{:T(128)}, /*index=5*/s32[]{:T(128)}, s32[]{:T(128)}) %tuple.52), condition=%wide.region_3.4_spmd, body=%wide.region_2.3_spmd.sunk | while | flops 131077 | bytes 2621575 | solution.py:37
  381.2 3.8 dynamic_update_slice.8
  388.9 3.8 dynamic_update_slice.8
  396.6 3.8 dynamic_update_slice.8
  404.4 3.8 dynamic_update_slice.8
  412.1 3.8 dynamic_update_slice.8
  419.8 3.8 dynamic_update_slice.8
  427.6 3.8 dynamic_update_slice.8
  435.3 3.8 dynamic_update_slice.8
  443.0 3.8 dynamic_update_slice.8
  450.7 3.8 dynamic_update_slice.8
  458.5 3.7 dynamic_update_slice.8
  466.1 3.8 dynamic_update_slice.8
  473.8 3.8 dynamic_update_slice.8
  481.6 3.8 dynamic_update_slice.8
  489.3 3.8 dynamic_update_slice.8
  497.0 3.8 dynamic_update_slice.8
  504.8 3.8 dynamic_update_slice.8
  512.5 3.8 dynamic_update_slice.8
  520.2 3.8 dynamic_update_slice.8
  527.9 3.8 dynamic_update_slice.8
  535.7 3.8 dynamic_update_slice.8
  543.4 3.8 dynamic_update_slice.8
  551.1 3.8 dynamic_update_slice.8
  558.9 3.8 dynamic_update_slice.8
  566.6 3.8 dynamic_update_slice.8
  574.3 3.8 dynamic_update_slice.8
  582.0 3.8 dynamic_update_slice.8
  589.8 3.8 dynamic_update_slice.8
  597.5 3.8 dynamic_update_slice.8
  605.2 3.8 dynamic_update_slice.8
  613.0 3.7 dynamic_update_slice.8
  620.6 3.8 dynamic_update_slice.8
  624.4 153.2 %all-gather.5.cloned.1.call-done = f32[1024,4096]{1,0:T(8,128)} async-done(((f32[256,4096]{1,0:T(8,128)}), f32[1024,4096]{1,0:T(8,128)}) %all-gather.5.cloned.1.call-update) | async-done | bytes 16777232 | tf_op jit(solution)/shard_map/all_gather | solution.py:40
  777.6 30.1 %convolution_bitcast_fusion = f32[256,4096]{0,1:T(8,128)} fusion(f32[1024,4096]{1,0:T(8,128)} %all-gather.5.cloned.1.call-done, f32[256,1024]{1,0:T(8,128)S(1)} %copy-done), kind=kOutput, calls=%fused_computation.5 | convolution fusion | flops 12884901888 | bytes 22020096 | tf_op jit(solution)/shard_map/dot_general | solution.py:38
  807.6 5.6 copy.19
  (179 shorter events, 168.7 us)
Async XLA Ops:
  6.5 771.0 %copy-start = (f32[256,1024]{1,0:T(8,128)S(1)}, f32[256,1024]{1,0:T(8,128)}, u32[]{:S(2)}) copy-start(f32[256,1024]{1,0:T(8,128)} %param.15) | copy-start | bytes 3145732
  6.5 4.8 copy-start.4
  6.5 112.7 %copy-start.2 = (s32[32,32]{1,0:T(8,128)S(1)}, s32[32,32]{1,0:T(8,128)}, u32[]{:S(2)}) copy-start(s32[32,32]{1,0:T(8,128)} %param.12) | copy-start | bytes 12292
  6.5 112.7 %copy-start.3 = (s32[96]{0:T(128)S(1)}, s32[96]{0:T(128)}, u32[]{:S(2)}) copy-start(s32[96]{0:T(128)} %param.13) | copy-start | bytes 1156
  6.5 267.4 %reduce-scatter.2.cloned.1.call-start = ((), (), s32[]{:S(2)}) async-start(), calls=%async_computation.1 | async-start | bytes 12976128 | tf_op jit(solution)/shard_map/reduce_scatter | solution.py:26
  167.2 106.7 %copy-start.1 = (f32[3,128,128]{2,1,0:T(8,128)S(1)}, f32[3,128,128]{2,1,0:T(8,128)}, u32[]{:S(2)}) copy-start(f32[3,128,128]{2,1,0:T(8,128)} %param.14) | copy-start | bytes 589828
  167.2 172.9 %all-gather.3.cloned.1.call-start = ((), (), s32[]{:S(2)}) async-start(), calls=%async_computation.2 | async-start | bytes 12976128 | tf_op jit(solution)/shard_map/all_gather | solution.py:28
  276.2 501.4 %all-gather.5.cloned.1.call-start = ((), (), s32[]{:S(2)}) async-start(), calls=%async_computation.3 | async-start | bytes 20971520 | tf_op jit(solution)/shard_map/all_gather | solution.py:40
Sparse Core Ops, SparseCore 0:
  167.3 106.5 reduce-scatter.1
  276.4 63.6 all-gather.2
  624.5 153.0 all-gather.4
where the time goes:
time: 833 us; the launch traced here: 820 us
  waiting for transfers between devices  324 us (39%)
  local copies, waits for them, and re-layouts  274 us (33%)
  matrix products  100 us (12%)
  loops' own time  61.3 us (7%)
  other arithmetic  47.4 us (6%)
  between operations  13.4 us (2%)
    all_gather x1, waiting for transfers between devices, per_device(): lax.all_gather(corrected, 'band', axis=0, tiled=True)  153 us
    dynamic_update_slice x32, local copies, waits for them, and re-layouts, add_window(): lax.dynamic_update_slice_in_dim(current, previous + updates[slot_index],...  120 us
    gather x96, local copies, waits for them, and re-layouts  108 us
    reduce_scatter x1, waiting for transfers between devices, per_device(): lax.psum_scatter(per_atom, 'dom', scatter_dimension=0, tiled=True)  107 us
    all_gather x1, waiting for transfers between devices, per_device(): all_factors = lax.all_gather(owned_factors, 'dom', axis=0, tiled=True)  63.9 us
    another operation x1, loops' own time, per_device(): corrected = lax.fori_loop(0, slot_count, add_window, orbitals)  61.3 us
    add x32, other arithmetic, add_window(): previous + updates[slot_index]  46.6 us
    dot_general x1, matrix products, per_device(): jnp.dot(rotation, lax.all_gather(corrected, 'band', axis=0, tiled=True),...  30.1 us
  transfers between devices with their start and end apart: 3, of which 3 were waited for; matrix products, arithmetic and copies ran while one was open for 0% of the time, Pallas kernels for 0%

commit v1 on v0

v1 whole, which is shorter than its diff:
```python
import functools

import jax
import jax.numpy as jnp
from jax import lax
from jax.experimental import pallas as pl
from jax.experimental.pallas import tpu as pltpu
from jax.sharding import PartitionSpec as P

HIGH = lax.Precision.HIGH
LANES = 128
GROUP = 4


def split(value):
    high = value.astype(jnp.bfloat16)
    low = (value - high.astype(jnp.float32)).astype(jnp.bfloat16)
    return high, low


def dot(a, b):
    return jnp.dot(a, b, preferred_element_type=jnp.float32)


def dot_nt(a, b):
    return lax.dot_general(a, b, (((1,), (1,)), ((), ())), preferred_element_type=jnp.float32)


def place(start, cells, wide):
    tile = jnp.minimum(start // LANES, (cells - wide) // LANES)
    return pl.multiple_of(tile * LANES, LANES), start - tile * LANES


def shifted(projector, pad, shift, window, wide):
    pad[pl.ds(LANES, window), :] = projector
    return split(pad[pl.ds(LANES - shift, wide), :])


def clear(pad, window):
    edge = jnp.zeros((LANES, pad.shape[1]), jnp.float32)
    pad[pl.ds(0, LANES), :] = edge
    pad[pl.ds(LANES + window, LANES), :] = edge


def project_kernel(dom, start, slot_atom, home, orbitals, projectors, sums, high, low, *pads):
    step = pl.program_id(0)
    group, window, _ = projectors.shape
    cells = orbitals.shape[1]
    wide = window + LANES

    @pl.when(step == 0)
    def _():
        for pad in pads:
            clear(pad, window)
        sums[...] = jnp.zeros_like(sums)
        value = orbitals[...]
        top, rest = split(value)
        high[...] = top
        low[...] = rest

    for k in range(group):
        slot = step * group + k
        row = home[slot_atom[dom[0], slot]]
        cell, shift = place(start[slot], cells, wide)
        p_high, p_low = shifted(projectors[k], pads[k], shift, window, wide)
        o_high = high[:, pl.ds(cell, wide)]
        o_low = low[:, pl.ds(cell, wide)]
        both = dot(o_high, jnp.concatenate([p_high, p_low], axis=1))
        projs = p_high.shape[1]
        sums[row] += both[:, :projs] + both[:, projs:] + dot(o_low, p_high)


def project(dom, start, slot_atom, home, orbitals, projectors):
    slots, window, projs = projectors.shape
    bands, cells = orbitals.shape
    atoms = home.shape[0]
    return pl.pallas_call(
        project_kernel,
        out_shape=jax.ShapeDtypeStruct((atoms, bands, projs), jnp.float32),
        grid_spec=pltpu.PrefetchScalarGridSpec(
            num_scalar_prefetch=4,
            grid=(slots // GROUP,),
            in_specs=[
                pl.BlockSpec((bands, cells), lambda i, *_: (0, 0), pipeline_mode=pl.Buffered(1)),
                pl.BlockSpec((GROUP, window, projs), lambda i, *_: (i, 0, 0)),
            ],
            out_specs=pl.BlockSpec(
                (atoms, bands, projs), lambda i, *_: (0, 0, 0), pipeline_mode=pl.Buffered(1)
            ),
            scratch_shapes=[pltpu.VMEM((bands, cells), jnp.bfloat16)] * 2
            + [pltpu.VMEM((window + 2 * LANES, projs), jnp.float32)] * GROUP,
        ),
        cost_estimate=pl.CostEstimate(
            flops=6 * slots * window * bands * projs, bytes_accessed=28 << 20, transcendentals=0
        ),
        compiler_params=pltpu.CompilerParams(vmem_limit_bytes=40 << 20),
        name="project",
    )(dom, start, slot_atom, home, orbitals, projectors)


def update_kernel(dom, start, slot_atom, home, *refs):
    group = GROUP
    factors = refs[:group]
    projectors, rotated, out = refs[group : group + 3]
    pads = refs[group + 3 :]
    step = pl.program_id(0)
    _, window, _ = projectors.shape
    cells = out.shape[1]
    wide = window + LANES

    @pl.when(step == 0)
    def _():
        for pad in pads:
            clear(pad, window)
        out[...] = rotated[...]

    for k in range(group):
        slot = step * group + k
        cell, shift = place(start[slot], cells, wide)
        p_high, p_low = shifted(projectors[k], pads[k], shift, window, wide)
        f_high, f_low = split(factors[k][0])
        update = dot_nt(
            jnp.concatenate([f_high, f_low, f_high], axis=1),
            jnp.concatenate([p_high, p_high, p_low], axis=1),
        )
        out[:, pl.ds(cell, wide)] += update


def update(dom, start, slot_atom, home, factors, projectors, rotated):
    slots, window, projs = projectors.shape
    bands, cells = rotated.shape

    def factor_spec(k):
        return pl.BlockSpec(
            (1, bands, projs),
            lambda i, d, s, a, h: (h[a[d[0], i * GROUP + k]], 0, 0),
        )

    return pl.pallas_call(
        update_kernel,
        out_shape=jax.ShapeDtypeStruct((bands, cells), jnp.float32),
        grid_spec=pltpu.PrefetchScalarGridSpec(
            num_scalar_prefetch=4,
            grid=(slots // GROUP,),
            in_specs=[factor_spec(k) for k in range(GROUP)]
            + [
                pl.BlockSpec((GROUP, window, projs), lambda i, *_: (i, 0, 0)),
                pl.BlockSpec((bands, cells), lambda i, *_: (0, 0), pipeline_mode=pl.Buffered(1)),
            ],
            out_specs=pl.BlockSpec(
                (bands, cells), lambda i, *_: (0, 0), pipeline_mode=pl.Buffered(1)
            ),
            scratch_shapes=[pltpu.VMEM((window + 2 * LANES, projs), jnp.float32)] * GROUP,
        ),
        cost_estimate=pl.CostEstimate(
            flops=6 * slots * window * bands * projs, bytes_accessed=20 << 20, transcendentals=0
        ),
        compiler_params=pltpu.CompilerParams(vmem_limit_bytes=40 << 20),
        name="update",
    )(dom, start, slot_atom, home, *([factors] * GROUP), projectors, rotated)


def per_device(orbitals, projectors, window_start, slot_atom, atom_home, atom_matrices, rotation):
    dom = lax.axis_index("dom").astype(jnp.int32).reshape(1)
    every = lax.all_gather(orbitals, "band", axis=0, tiled=True)
    sums = project(dom, window_start, slot_atom, atom_home, orbitals, projectors)
    owned = lax.psum_scatter(sums, "dom", scatter_dimension=0, tiled=True)
    owned = lax.all_gather(owned, "band", axis=1, tiled=True)
    owned = jnp.einsum("cb,abp->acp", rotation, owned, precision=HIGH)
    owned = jnp.einsum("acp,apq->acq", owned, atom_matrices, precision=HIGH)
    factors = lax.all_gather(owned, "dom", axis=0, tiled=True)
    rotated = jnp.dot(rotation, every, precision=HIGH, preferred_element_type=jnp.float32)
    return update(dom, window_start, slot_atom, atom_home, factors, projectors, rotated)


def solution(mesh):
    in_specs = (
        P("band", "dom"),
        P("dom", None, None),
        P("dom"),
        P(),
        P(),
        P("dom", None, None),
        P("band", None),
    )
    out_specs = P("band", "dom")
    return jax.shard_map(
        per_device, mesh=mesh, in_specs=in_specs, out_specs=out_specs, check_vma=False
    )
```

time: 833 us -> 413 us (0.50); the launches traced: 820 us -> 413 us
  local copies, waits for them, and re-layouts: 274 us -> 13.3 us
  matrix products: 100 us -> 16.8 us
  loops' own time: 61.3 us -> 0 us
  other arithmetic: 47.4 us -> 0 us
  Pallas kernels: 0 us -> 28.4 us
  waiting for transfers between devices: 324 us -> 341 us
    dynamic_update_slice x32 -> x0, local copies, waits for them, and re-layouts: 120 us -> none  [add_window(): lax.dynamic_update_slice_in_dim(current, previous + updates[slot_index],...]
    gather x96 -> x0, local copies, waits for them, and re-layouts: 108 us -> none
    dot_general x6 -> x3, matrix products: 100 us -> 16.8 us  [the longest x1 13.3 us: per_device(): jnp.dot(rotation, every, precision=HIGH, preferred_element_type=jnp.float32)]
    another operation x2 -> x0, loops' own time: 61.3 us -> none  [the longest x1 61.3 us: per_device(): corrected = lax.fori_loop(0, slot_count, add_window, orbitals)]
    add x32 -> x0, other arithmetic: 46.6 us -> none  [add_window(): previous + updates[slot_index]]
    pallas_call x0 -> x2, Pallas kernels: none -> 28.4 us  [the longest x1 14.8 us: project(): pl.pallas_call(project_kernel, out_shape=jax.ShapeDtypeStruct((atoms, ban...]
    dot_general x2 -> x0, local copies, waits for them, and re-layouts: 22 us -> none  [the longest x1 16.4 us: per_device(): jnp.einsum('rs,sbp->rbp', home_match, partials, precision=HIGHEST)]
    dynamic_slice x32 -> x0, local copies, waits for them, and re-layouts: 19.3 us -> none  [add_window(): offset = window_start[slot_index]]
  transfers between devices with their start and end apart: 3 -> 4, of which waited for: 3 -> 4; matrix products, arithmetic and copies ran while one was open for 0% -> 4% of each run, Pallas kernels for 0% -> 0%
where the time goes in v1:
time: 413 us
  waiting for transfers between devices  341 us (83%)
  Pallas kernels  28.4 us (7%)
  matrix products  16.8 us (4%)
  local copies, waits for them, and re-layouts  13.3 us (3%)
  between operations  13.2 us (3%)
    all_gather x1, waiting for transfers between devices, per_device(): every = lax.all_gather(orbitals, 'band', axis=0, tiled=True)  152 us
    reduce_scatter x1, waiting for transfers between devices, per_device(): owned = lax.psum_scatter(sums, 'dom', scatter_dimension=0, tiled=True)  107 us
    all_gather x1, waiting for transfers between devices, per_device(): factors = lax.all_gather(owned, 'dom', axis=0, tiled=True)  53.5 us
    all_gather x1, waiting for transfers between devices, per_device(): owned = lax.all_gather(owned, 'band', axis=1, tiled=True)  27.9 us
    pallas_call x1, Pallas kernels, project(): pl.pallas_call(project_kernel, out_shape=jax.ShapeDtypeStruct((atoms, ban...  14.8 us
    pallas_call x1, Pallas kernels, update(): pl.pallas_call(update_kernel, out_shape=jax.ShapeDtypeStruct((bands, cell...  13.6 us
    dot_general x1, matrix products, per_device(): jnp.dot(rotation, every, precision=HIGH, preferred_element_type=jnp.float32)  13.3 us
    unnamed x24, local copies, waits for them, and re-layouts  13.3 us
  transfers between devices with their start and end apart: 4, of which 4 were waited for; matrix products, arithmetic and copies ran while one was open for 4% of the time, Pallas kernels for 0%

profile of v1, /device:TPU:1, one launch (start us, length us, event | category | flops | bytes accessed | tf_op | source)
XLA Modules:
  0.0 412.9 jit_solution(11563905283603884707)
XLA Ops:
  6.5 0.0 copy-start
  6.5 0.0 reduce-scatter.2.cloned.1.call-start
  6.5 0.0 copy-start.1
  6.5 3.5 copy-done.1
  10.0 0.0 copy-start.3
  10.0 2.2 copy-done.3
  12.2 0.0 copy-start.5
  12.2 0.7 copy-done.5
  12.9 0.0 copy-start.7
  12.9 0.7 copy-done.7
  13.6 0.0 copy-start.9
  13.6 0.7 copy-done.9
  14.2 14.8 %project.1 = f32[96,256,128]{2,1,0:T(8,128)} custom-call(s32[1]{0:T(128)} %bitcast.dom, s32[32]{0:T(128)S(1)} %copy-done.7, s32[32,32]{1,0:T(8,128)S(1)} %copy-done.5, s32[96]{0:T(128)S(1)} %copy-done.9, f32[256,4096]{1,0:T(8,128)S(1)} %copy-done.3, f32[32,512,128]{2,1,0:T(8,128)S(1)} %copy-done.1), custom_call_target="tpu_custom_call" | custom-call | flops 3221225472 | bytes 29360128 | tf_op jit(solution)/shard_map/project/pallas_call | solution.py:77
  29.0 0.0 reduce-scatter.2.cloned.1.call-update
  29.0 0.0 copy-start.11
  29.0 0.0 all-gather.4.cloned.1.call-start
  29.1 106.7 %reduce-scatter.2.cloned.1.call-done = f32[3,256,128]{2,1,0:T(8,128)} async-done(((f32[96,256,128]{2,1,0:T(8,128)}), f32[3,256,128]{2,1,0:T(8,128)}) %reduce-scatter.2.cloned.1.call-update) | async-done | bytes 393232 | tf_op jit(solution)/shard_map/reduce_scatter | solution.py:167
  135.8 0.0 all-gather.4.cloned.1.call-update
  135.8 0.0 all-gather.8.cloned.1.call-start
  135.8 0.7 all-gather.8.cloned.1.call-update
  136.5 0.0 all-gather.6.cloned.1.call-start
  136.6 27.9 %all-gather.4.cloned.1.call-done = f32[3,1024,128]{2,1,0:T(8,128)} async-done(((f32[3,256,128]{2,1,0:T(8,128)}), f32[3,1024,128]{2,1,0:T(8,128)}) %all-gather.4.cloned.1.call-update) | async-done | bytes 1572880 | tf_op jit(solution)/shard_map/all_gather | solution.py:168
  164.4 0.0 copy-done
  164.4 2.4 fusion
  166.8 0.0 copy-done.11
  166.8 1.1 fusion.2
  167.9 0.0 all-gather.6.cloned.1.call-update
  168.0 0.0 copy-start.6
  168.0 0.0 copy-start.8
  168.0 0.0 copy-start.10
  168.0 152.4 %all-gather.8.cloned.1.call-done = f32[1024,4096]{1,0:T(8,128)} async-done(((f32[256,4096]{1,0:T(8,128)}), f32[1024,4096]{1,0:T(8,128)}) %all-gather.8.cloned.1.call-update) | async-done | bytes 16777232 | tf_op jit(solution)/shard_map/all_gather | solution.py:165
  320.4 13.3 %fusion.3.refs_5_ = f32[256,4096]{1,0:T(8,128)} fusion(f32[256,1024]{1,0:T(8,128)S(1)} %copy-done, f32[1024,4096]{1,0:T(8,128)} %all-gather.8.cloned.1.call-done), kind=kOutput, calls=%fused_computation.3 | convolution fusion | flops 6442450944 | bytes 22020096 | tf_op jit(solution)/shard_map/dot_general | solution.py:172
  333.6 53.5 %all-gather.6.cloned.1.call-done.refs_0_.refs_1_.refs_2_.refs_3_ = f32[96,256,128]{2,1,0:T(8,128)} async-done(((f32[3,256,128]{2,1,0:T(8,128)}), f32[96,256,128]{2,1,0:T(8,128)}) %all-gather.6.cloned.1.call-update) | async-done | bytes 12582928 | tf_op jit(solution)/shard_map/all_gather | solution.py:171
  387.1 0.0 copy-done.6
  387.1 0.0 copy-done.8
  387.1 0.0 copy-done.10
  387.1 0.0 copy-start.2
  387.1 3.4 copy-done.2
  390.5 0.0 copy-start.4
  390.5 2.2 copy-done.4
  392.7 13.6 %update.1 = f32[256,4096]{1,0:T(8,128)} custom-call(s32[1]{0:T(128)} %bitcast.dom, s32[32]{0:T(128)S(1)} %copy-done.8, s32[32,32]{1,0:T(8,128)S(1)} %copy-done.6, s32[96]{0:T(128)S(1)} %copy-done.10, f32[96,256,128]{2,1,0:T(8,128)} %all-gather.6.cloned.1.call-done.refs_0_.refs_1_.refs_2_.refs_3_, ...), custom_call_target="tpu_custom_call" | custom-call | flops 3221225472 | bytes 20971520 | tf_op jit(solution)/shard_map/update/pallas_call | solution.py:139
Async XLA Ops:
  6.5 157.9 %copy-start = (f32[256,1024]{1,0:T(8,128)S(1)}, f32[256,1024]{1,0:T(8,128)}, u32[]{:S(2)}) copy-start(f32[256,1024]{1,0:T(8,128)} %param.13) | copy-start | bytes 3145732
  6.5 129.2 %reduce-scatter.2.cloned.1.call-start = ((), (), s32[]{:S(2)}) async-start(), calls=%async_computation.1 | async-start | bytes 12976128 | tf_op jit(solution)/shard_map/reduce_scatter | solution.py:167
  6.5 3.5 copy-start.1
  10.0 2.2 copy-start.3
  12.2 0.7 copy-start.5
  12.9 0.7 copy-start.7
  13.6 0.7 copy-start.9
  29.0 137.8 %copy-start.11 = (f32[3,128,128]{2,1,0:T(8,128)S(1)}, f32[3,128,128]{2,1,0:T(8,128)}, u32[]{:S(2)}) copy-start(f32[3,128,128]{2,1,0:T(8,128)} %param.12) | copy-start | bytes 589828
  29.0 135.4 %all-gather.4.cloned.1.call-start = ((), (), s32[]{:S(2)}) async-start(), calls=%async_computation.2 | async-start | bytes 1966080 | tf_op jit(solution)/shard_map/all_gather | solution.py:168
  135.8 184.6 %all-gather.8.cloned.1.call-start = ((), (), s32[]{:S(2)}) async-start(), calls=%async_computation.4 | async-start | bytes 20971520 | tf_op jit(solution)/shard_map/all_gather | solution.py:165
  136.5 250.6 %all-gather.6.cloned.1.call-start = ((), (), s32[]{:S(2)}) async-start(), calls=%async_computation.3 | async-start | bytes 12976128 | tf_op jit(solution)/shard_map/all_gather | solution.py:171
  168.0 219.2 %copy-start.6 = (s32[32,32]{1,0:T(8,128)S(1)}, s32[32,32]{1,0:T(8,128)}, u32[]{:S(2)}) copy-start(s32[32,32]{1,0:T(8,128)} %slot_atom.3) | copy-start | bytes 12292
  168.0 219.1 %copy-start.8 = (s32[32]{0:T(128)S(1)}, s32[32]{0:T(128)}, u32[]{:S(2)}) copy-start(s32[32]{0:T(128)} %start.3) | copy-start | bytes 388
  168.0 219.1 %copy-start.10 = (s32[96]{0:T(128)S(1)}, s32[96]{0:T(128)}, u32[]{:S(2)}) copy-start(s32[96]{0:T(128)} %home.3) | copy-start | bytes 1156
  387.1 3.4 copy-start.2
  390.5 2.2 copy-start.4
Sparse Core Ops, SparseCore 0:
  29.1 106.5 reduce-scatter.1
  137.5 26.8 all-gather.3
  166.2 154.1 all-gather.7
  322.7 64.3 all-gather.5

commit v2 on v1

--- a/solution.py
+++ b/solution.py
@@ -1,5 +1,3 @@
-import functools
-
 import jax
 import jax.numpy as jnp
 from jax import lax
@@ -7,7 +5,6 @@
 from jax.experimental.pallas import tpu as pltpu
 from jax.sharding import PartitionSpec as P
 
-HIGH = lax.Precision.HIGH
 LANES = 128
 GROUP = 4
 
@@ -160,16 +157,416 @@
     )(dom, start, slot_atom, home, *([factors] * GROUP), projectors, rotated)
 
 
+MESH = pl.DeviceIdType.MESH
+RING = 4
+ORDER = (2, 1, 3, 0)
+
+
+def ring(position, offset):
+    return lax.rem(position + offset, RING)
+
+
+def tile_of(index, size):
+    return pl.ds(pl.multiple_of(index * size, size), size)
+
+
+class Links:
+    def __init__(self):
+        self.band = lax.axis_index("band")
+        dom = lax.axis_index("dom")
+        self.core = lax.rem(dom, 2)
+        self.z = lax.rem(dom // 2, RING)
+        self.x = dom // (2 * RING)
+
+    def place(self, band, x, z, core):
+        return (band, (x * RING + z) * 2 + core)
+
+    def at_band(self, offset):
+        return self.place(ring(self.band, offset), self.x, self.z, self.core)
+
+    def at_x(self, offset):
+        return self.place(self.band, ring(self.x, offset), self.z, self.core)
+
+    def at_z(self, offset):
+        return self.place(self.band, self.x, ring(self.z, offset), self.core)
+
+    def partner(self):
+        return self.place(self.band, self.x, self.z, 1 - self.core)
+
+
+def exchange_kernel(
+    sums, orbitals, rotation, matrices, factors, rotated,
+    cells_in, cells_out, full, r_high, r_low, total, mate, hop1, hop2, hop3, hop4, gathered, owned,
+    sem_load, sem_keep, sem_own, *sems
+):
+    link = Links()
+    b, x, z, c = link.band, link.x, link.z, link.core
+    names = ("yin", "yout", "r1", "r2", "r3", "s0", "one", "two", "sum", "ag1", "ag2", "agf", "core")
+    send = dict(zip(names, sems[0::2]))
+    recv = dict(zip(names, sems[1::2]))
+    bands, cells = orbitals.shape
+    quarter = cells // RING
+    parts = cells_in.shape[0]
+    width = quarter // parts
+    half = bands // 2
+    sub = half // 2
+    started = []
+
+    def push(src, dst, kind, index, device):
+        copy = pltpu.make_async_remote_copy(
+            src_ref=src, dst_ref=dst, send_sem=send[kind].at[index], recv_sem=recv[kind].at[index],
+            device_id=device, device_id_type=MESH,
+        )
+        copy.start()
+        started.append(copy)
+        return copy
+
+    def keep(src, dst, sem):
+        copy = pltpu.make_async_copy(src, dst, sem)
+        copy.start()
+        return copy
+
+    barrier = pltpu.get_barrier_semaphore()
+    peers = [f(o) for f in (link.at_band, link.at_x, link.at_z) for o in (1, 2, 3)] + [link.partner()]
+    for peer in peers:
+        pl.semaphore_signal(barrier, inc=1, device_id=peer, device_id_type=MESH)
+    pl.semaphore_wait(barrier, len(peers))
+
+    first = (x, z)
+    second = (z, x)
+    at_first = (link.at_x, link.at_z)
+    at_second = (link.at_z, link.at_x)
+
+    def sums_at(h, t, core):
+        rows = pl.ds(h * half, half)
+        if h == 0:
+            return sums.at[t, :, core, :, rows, :]
+        return sums.at[:, t, core, :, rows, :]
+
+    def factor_at(h, t, u, core, low=0, size=None):
+        rows = pl.ds(h * half + low, half if size is None else size)
+        if h == 0:
+            return factors.at[t, u, core, :, rows, :]
+        return factors.at[u, t, core, :, rows, :]
+
+    mates, loads = {}, {}
+    for o in ORDER:
+        for h in range(2):
+            t = ring(first[h], o)
+            mates[h, o] = push(sums_at(h, t, 1 - c), mate.at[h, t], "s0", (h, o), link.partner())
+            loads[h, o] = keep(sums_at(h, t, c), total.at[h, t], sem_load.at[h, o])
+    r1 = {}
+    for o in (1, 2, 3):
+        for h in range(2):
+            piece = (h, first[h], c)
+            r1[o, h] = push(rotation.at[piece], full.at[(b,) + piece], "r1", (o - 1, h), link.at_band(o))
+    own_rows = keep(rotation, full.at[b], sem_own.at[0])
+    yin, own_cells = {}, []
+    for i in range(parts):
+        for o in (1, 2, 3):
+            src = orbitals.at[:, tile_of(ring(b, o) * parts + i, width)]
+            yin[i, o] = push(src, cells_in.at[i, b], "yin", (i, o - 1), link.at_band(o))
+        own_cells.append(keep(orbitals.at[:, tile_of(b * parts + i, width)], cells_in.at[i, b], sem_keep.at[i]))
+
+    one, two = {}, {}
+
+    def gather_mate(h, o):
+        t = ring(first[h], o)
+        loads[h, o].wait()
+        mates[h, o].wait_recv()
+
+        def body(u, carry):
+            total[h, t, u] += mate[h, t, u]
+            return carry
+
+        lax.fori_loop(0, RING, body, 0)
+
+    low2, high2 = pl.ds(0, 2), pl.ds(2, 2)
+    for h in range(2):
+        gather_mate(h, 2)
+        t = ring(first[h], 2)
+        one[h, 0, 0] = push(total.at[h, t, low2], hop1.at[h, 0], "one", (h, 0, 0), at_first[h](1))
+        one[h, 1, 0] = push(total.at[h, t, high2], hop1.at[h, 1], "one", (h, 1, 0), at_first[h](3))
+    for h in range(2):
+        gather_mate(h, 1)
+        t = ring(first[h], 1)
+        one[h, 0, 1] = push(total.at[h, t, high2], hop2.at[h, 0, high2], "one", (h, 0, 1), at_first[h](1))
+        gather_mate(h, 3)
+        t = ring(first[h], 3)
+        one[h, 1, 1] = push(total.at[h, t, low2], hop2.at[h, 1, low2], "one", (h, 1, 1), at_first[h](3))
+
+    r2 = {}
+    for o in (1, 2, 3):
+        k = ring(b, RING - o)
+        for h in range(2):
+            r1[o, h].wait_recv()
+            piece = (k, h, first[h], c)
+            for p in (1, 2, 3):
+                r2[o, p, h] = push(full.at[piece], full.at[piece], "r2", (o - 1, p - 1, h), at_first[h](p))
+
+    for h in range(2):
+        gather_mate(h, 0)
+
+    def add_rows(h, t, start, source):
+        def body(u, carry):
+            total[h, t, start + u] += source[h, start // 2, u]
+            return carry
+
+        lax.fori_loop(0, 2, body, 0)
+
+    for h in range(2):
+        one[h, 0, 0].wait_recv()
+        t = ring(first[h], 1)
+        add_rows(h, t, 0, hop1)
+        one[h, 0, 2] = push(total.at[h, t, low2], hop2.at[h, 0, low2], "one", (h, 0, 2), at_first[h](1))
+        one[h, 1, 0].wait_recv()
+        t = ring(first[h], 3)
+        add_rows(h, t, 2, hop1)
+        one[h, 1, 2] = push(total.at[h, t, high2], hop2.at[h, 1, high2], "one", (h, 1, 2), at_first[h](3))
+
+    r3 = {}
+    for o in (1, 2, 3):
+        k = ring(b, RING - o)
+        for h in range(2):
+            for p in (1, 2, 3):
+                r2[o, p, h].wait_recv()
+        mine = full.at[k, :, :, c]
+        r3[o] = push(mine, mine, "r3", (o - 1,), link.partner())
+
+    own_rows.wait()
+    for o in (1, 2, 3):
+        r3[o].wait_recv()
+
+    def split_rows(k, carry):
+        top, rest = split(full[k].reshape(bands, full.shape[-1]))
+        r_high[k] = top
+        r_low[k] = rest
+        return carry
+
+    lax.fori_loop(0, RING, split_rows, 0)
+
+    yout, own_out = {}, []
+
+    def rotate(i):
+        for o in (1, 2, 3):
+            yin[i, o].wait_recv()
+        own_cells[i].wait()
+        high, low = split(cells_in[i].reshape(RING * bands, width))
+        pair = jnp.concatenate([high, low], axis=1)
+
+        def body(k, carry):
+            both = dot(r_high[k], pair)
+            cells_out[i, k] = both[:, :width] + both[:, width:] + dot(r_low[k], high)
+            return carry
+
+        lax.fori_loop(0, RING, body, 0)
+        columns = tile_of(b * parts + i, width)
+        for o in (1, 2, 3):
+            src = cells_out.at[i, ring(b, o)]
+            yout[i, o] = push(src, rotated.at[:, columns], "yout", (i, o - 1), link.at_band(o))
+        own_out.append(keep(cells_out.at[i, b], rotated.at[:, columns], sem_keep.at[parts + i]))
+
+    rotate(0)
+
+    for h in range(2):
+        t = first[h]
+        one[h, 0, 1].wait_recv()
+        one[h, 1, 1].wait_recv()
+        one[h, 0, 2].wait_recv()
+        one[h, 1, 2].wait_recv()
+
+        def finish(u, carry, h=h, t=t):
+            total[h, t, u] += hop2[h, 0, u] + hop2[h, 1, u]
+            return carry
+
+        lax.fori_loop(0, RING, finish, 0)
+        lower, upper = pl.ds(0, sub), pl.ds(sub, sub)
+        s = second[h]
+        far, nxt, prv = ring(s, 2), ring(s, 1), ring(s, 3)
+        two[h, 0, 0] = push(total.at[h, t, far, :, lower], hop3.at[h, 0], "two", (h, 0, 0), at_second[h](1))
+        two[h, 1, 0] = push(total.at[h, t, far, :, upper], hop3.at[h, 1], "two", (h, 1, 0), at_second[h](3))
+        two[h, 0, 1] = push(
+            total.at[h, t, nxt, :, upper], hop4.at[h, 0, :, upper], "two", (h, 0, 1), at_second[h](1)
+        )
+        two[h, 1, 1] = push(
+            total.at[h, t, prv, :, lower], hop4.at[h, 1, :, lower], "two", (h, 1, 1), at_second[h](3)
+        )
+
+    for h in range(2):
+        t, s = first[h], second[h]
+        nxt, prv = ring(s, 1), ring(s, 3)
+        two[h, 0, 0].wait_recv()
+        total[h, t, nxt, :, lower] += hop3[h, 0]
+        two[h, 0, 2] = push(
+            total.at[h, t, nxt, :, lower], hop4.at[h, 0, :, lower], "two", (h, 0, 2), at_second[h](1)
+        )
+        two[h, 1, 0].wait_recv()
+        total[h, t, prv, :, upper] += hop3[h, 1]
+        two[h, 1, 2] = push(
+            total.at[h, t, prv, :, upper], hop4.at[h, 1, :, upper], "two", (h, 1, 2), at_second[h](3)
+        )
+
+    rotate(1)
+
+    for h in range(2):
+        t, s = first[h], second[h]
+        for d in range(2):
+            two[h, d, 1].wait_recv()
+            two[h, d, 2].wait_recv()
+        gathered[b, :, pl.ds(h * half, half), :] = total[h, t, s] + hop4[h, 0] + hop4[h, 1]
+    swap = {}
+    for o in (1, 2, 3):
+        swap[o] = push(gathered.at[b], gathered.at[b], "sum", (o - 1,), link.at_band(o))
+
+    rotate(2)
+
+    for o in (1, 2, 3):
+        swap[o].wait_recv()
+    projs = matrices.shape[-1]
+    for atom in range(matrices.shape[0]):
+        high, low = split(gathered[:, atom].reshape(RING * bands, projs))
+        both = dot(r_high[b], jnp.concatenate([high, low], axis=1))
+        turned = both[:, :projs] + both[:, projs:] + dot(r_low[b], high)
+        t_high, t_low = split(turned)
+        m_high, m_low = split(matrices[atom])
+        both = dot(t_high, jnp.concatenate([m_high, m_low], axis=1))
+        owned[atom] = both[:, :projs] + both[:, projs:] + dot(t_low, m_high)
+
+    own_factor = keep(owned, factors.at[x, z, c], sem_own.at[1])
+    mate_core = []
+
+    def to_mate(src, h, t, u, index):
+        mate_core.append(push(src, factor_at(h, t, u, c), "core", (h, index), link.partner()))
+
+    ag1, ag2, agf = {}, {}, {}
+    for h in range(2):
+        t, s = first[h], second[h]
+        for d, peer, order in ((0, 1, (0, 1)), (1, 3, (1, 0))):
+            for m, part in enumerate(order):
+                rows = pl.ds(h * half + part * sub, sub)
+                ag1[h, d, m] = push(
+                    owned.at[:, rows], factor_at(h, t, s, c, part * sub, sub), "ag1", (h, d, m), at_second[h](peer)
+                )
+    def spread(h, r, src, u):
+        t = first[h]
+        for d, peer in ((0, 1), (1, 3)):
+            ag2[h, d, r] = push(src, factor_at(h, t, u, c), "ag2", (h, d, r), at_first[h](peer))
+        to_mate(src, h, t, u, r)
+
+    lines = (0, 3, 1, 2)
+    for h in range(2):
+        spread(h, 0, owned.at[:, pl.ds(h * half, half)], second[h])
+    for h in range(2):
+        t, s = first[h], second[h]
+        for d, back, peer in ((0, 3, 1), (1, 1, 3)):
+            ag1[h, d, 0].wait_recv()
+            piece = factor_at(h, t, ring(s, back), c, d * sub, sub)
+            ag1[h, d, 2] = push(piece, piece, "ag1", (h, d, 2), at_second[h](peer))
+    for h in range(2):
+        t, s = first[h], second[h]
+        for d, r in ((0, 1), (1, 2)):
+            ag1[h, d, 1].wait_recv()
+            u = ring(s, lines[r])
+            spread(h, r, factor_at(h, t, u, c), u)
+    for h in range(2):
+        t, s = first[h], second[h]
+        ag1[h, 0, 2].wait_recv()
+        ag1[h, 1, 2].wait_recv()
+        u = ring(s, 2)
+        spread(h, 3, factor_at(h, t, u, c), u)
+
+    rotate(3)
+
+    for r in range(RING):
+        for h in range(2):
+            u = ring(second[h], lines[r])
+            for d, back, peer in ((0, 3, 1), (1, 1, 3)):
+                ag2[h, d, r].wait_recv()
+                t = ring(first[h], back)
+                piece = factor_at(h, t, u, c)
+                if (r < 2) == (d == 0):
+                    agf[h, r] = push(piece, piece, "agf", (h, r), at_first[h](peer))
+                to_mate(piece, h, t, u, RING * (1 + d) + r)
+    for r in range(RING):
+        for h in range(2):
+            u = ring(second[h], lines[r])
+            agf[h, r].wait_recv()
+            t = ring(first[h], 2)
+            to_mate(factor_at(h, t, u, c), h, t, u, RING * 3 + r)
+
+    for copy in mate_core:
+        copy.wait_recv()
+    for copy in yout.values():
+        copy.wait_recv()
+    for copy in own_out:
+        copy.wait()
+    own_factor.wait()
+    for copy in started:
+        copy.wait_send()
+
+
+PARTS = 4
+
+
+def exchange(sums, orbitals, rotation, matrices):
+    atoms, bands, projs = sums.shape
+    cells = orbitals.shape[1]
+    all_bands = rotation.shape[1]
+    group = atoms // (2 * RING * RING)
+    width = cells // RING // PARTS
+    half = bands // 2
+    sub = half // 2
+    rows = bands // (4 * RING)
+    f32, bf16 = jnp.float32, jnp.bfloat16
+    counts = [
+        (PARTS, 3), (PARTS, 3), (3, 2), (3, 3, 2), (3,), (2, RING), (2, 2, 3), (2, 2, 3), (3,),
+        (2, 2, 3), (2, 2, RING), (2, RING), (2, 4 * RING),
+    ]
+    dma = pltpu.SemaphoreType.DMA
+    factors, rotated = pl.pallas_call(
+        exchange_kernel,
+        out_shape=(
+            jax.ShapeDtypeStruct((RING, RING, 2, group, bands, projs), f32),
+            jax.ShapeDtypeStruct((bands, cells), f32),
+        ),
+        in_specs=[pl.BlockSpec(memory_space=pl.ANY)] * 3 + [pl.BlockSpec(memory_space=pltpu.VMEM)],
+        out_specs=[pl.BlockSpec(memory_space=pl.ANY)] * 2,
+        scratch_shapes=[
+            pltpu.VMEM((PARTS, RING, bands, width), f32),
+            pltpu.VMEM((PARTS, RING, bands, width), f32),
+            pltpu.VMEM((RING, 2, RING, 2, rows, all_bands), f32),
+            pltpu.VMEM((RING, bands, all_bands), bf16),
+            pltpu.VMEM((RING, bands, all_bands), bf16),
+            pltpu.VMEM((2, RING, RING, group, half, projs), f32),
+            pltpu.VMEM((2, RING, RING, group, half, projs), f32),
+            pltpu.VMEM((2, 2, 2, group, half, projs), f32),
+            pltpu.VMEM((2, 2, RING, group, half, projs), f32),
+            pltpu.VMEM((2, 2, group, sub, projs), f32),
+            pltpu.VMEM((2, 2, group, half, projs), f32),
+            pltpu.VMEM((RING, group, bands, projs), f32),
+            pltpu.VMEM((group, bands, projs), f32),
+            dma((2, RING)),
+            dma((2 * PARTS,)),
+            dma((2,)),
+        ]
+        + [dma(shape) for shape in counts for _ in range(2)],
+        compiler_params=pltpu.CompilerParams(
+            collective_id=0, has_side_effects=True, vmem_limit_bytes=52 << 20
+        ),
+        name="exchange",
+    )(
+        sums.reshape(RING, RING, 2, group, bands, projs),
+        orbitals,
+        rotation.reshape(2, RING, 2, rows, all_bands),
+        matrices,
+    )
+    return factors.reshape(atoms, bands, projs), rotated
+
+
 def per_device(orbitals, projectors, window_start, slot_atom, atom_home, atom_matrices, rotation):
     dom = lax.axis_index("dom").astype(jnp.int32).reshape(1)
-    every = lax.all_gather(orbitals, "band", axis=0, tiled=True)
     sums = project(dom, window_start, slot_atom, atom_home, orbitals, projectors)
-    owned = lax.psum_scatter(sums, "dom", scatter_dimension=0, tiled=True)
-    owned = lax.all_gather(owned, "band", axis=1, tiled=True)
-    owned = jnp.einsum("cb,abp->acp", rotation, owned, precision=HIGH)
-    owned = jnp.einsum("acp,apq->acq", owned, atom_matrices, precision=HIGH)
-    factors = lax.all_gather(owned, "dom", axis=0, tiled=True)
-    rotated = jnp.dot(rotation, every, precision=HIGH, preferred_element_type=jnp.float32)
+    factors, rotated = exchange(sums, orbitals, rotation, atom_matrices)
     return update(dom, window_start, slot_atom, atom_home, factors, projectors, rotated)
 
 

time: 413 us -> 180 us (0.44)
  waiting for transfers between devices: 341 us -> 0 us
  Pallas kernels: 28.4 us -> 170 us
  matrix products: 16.8 us -> 0 us
  between operations: 13.2 us -> 0.08 us
    all_gather x3 -> x0, waiting for transfers between devices: 234 us -> none  [the longest x1 152 us: per_device(): every = lax.all_gather(orbitals, 'band', axis=0, tiled=True)]
    pallas_call x0 -> x1, Pallas kernels: none -> 141 us  [exchange(): pl.pallas_call(exchange_kernel, out_shape=(jax.ShapeDtypeStruct((RING, RI...]
    reduce_scatter x1 -> x0, waiting for transfers between devices: 107 us -> none  [per_device(): owned = lax.psum_scatter(sums, 'dom', scatter_dimension=0, tiled=True)]
    dot_general x3 -> x0, matrix products: 16.8 us -> none  [the longest x1 13.3 us: per_device(): jnp.dot(rotation, every, precision=HIGH, preferred_element_type=jnp.float32)]
  transfers between devices with their start and end apart: 4 -> 0, of which waited for: 4 -> 0; matrix products, arithmetic and copies ran while one was open for 4% -> 0% of each run, Pallas kernels for 0% -> 0%
where the time goes in v2:
time: 180 us; the launch traced here: 179 us
  Pallas kernels  170 us (94%)
  local copies, waits for them, and re-layouts  9.8 us (5%)
    pallas_call x1, Pallas kernels, exchange(): pl.pallas_call(exchange_kernel, out_shape=(jax.ShapeDtypeStruct((RING, RI...  141 us
    pallas_call x1, Pallas kernels, project(): pl.pallas_call(project_kernel, out_shape=jax.ShapeDtypeStruct((atoms, ban...  14.8 us
    pallas_call x1, Pallas kernels, update(): pl.pallas_call(update_kernel, out_shape=jax.ShapeDtypeStruct((bands, cell...  13.6 us
    unnamed x24, local copies, waits for them, and re-layouts  9.8 us

profile of v2, /device:TPU:1, one launch (start us, length us, event | category | flops | bytes accessed | tf_op | source)
XLA Modules:
  0.0 179.4 jit_solution(5829887215111397485)
XLA Ops:
  0.0 0.0 copy-start
  0.0 3.4 %copy-done = f32[32,512,128]{2,1,0:T(8,128)S(1)} copy-done((f32[32,512,128]{2,1,0:T(8,128)S(1)}, f32[32,512,128]{2,1,0:T(8,128)}, u32[]{:S(2)}) %copy-start) | copy-done | bytes 8388632
  3.4 0.0 copy-start.2
  3.4 2.2 %copy-done.2 = f32[256,4096]{1,0:T(8,128)S(1)} copy-done((f32[256,4096]{1,0:T(8,128)S(1)}, f32[256,4096]{1,0:T(8,128)}, u32[]{:S(2)}) %copy-start.2) | copy-done | bytes 4194328
  5.6 0.0 copy-start.6
  5.6 0.7 copy-done.6
  6.3 0.0 copy-start.8
  6.3 0.7 copy-done.8
  6.9 0.0 copy-start.10
  6.9 0.7 copy-done.10
  7.6 0.0 copy-start.4
  7.6 0.0 copy-start.5
  7.6 14.8 %project.1 = f32[96,256,128]{2,1,0:T(8,128)} custom-call(s32[1]{0:T(128)} %bitcast.dom, s32[32]{0:T(128)S(1)} %copy-done.8, s32[32,32]{1,0:T(8,128)S(1)} %copy-done.6, s32[96]{0:T(128)S(1)} %copy-done.10, f32[256,4096]{1,0:T(8,128)S(1)} %copy-done.2, f32[32,512,128]{2,1,0:T(8,128)S(1)} %copy-done), custom_call_target="tpu_custom_call" | custom-call | flops 3221225472 | bytes 29360128 | tf_op jit(solution)/shard_map/project/pallas_call | solution.py:74
  22.5 0.0 copy-done.4
  22.5 0.0 copy-done.5
  22.5 0.0 copy-start.1
  22.5 0.0 copy-start.7
  22.5 0.0 copy-start.9
  22.5 0.0 copy-start.11
  22.5 141.1 %exchange.1 = (f32[4,4,2,3,256,128]{5,4,3,2,1,0:T(8,128)}, f32[256,4096]{1,0:T(8,128)}) custom-call(f32[4,4,2,3,256,128]{5,4,3,2,1,0:T(8,128)} %bitcast.9, f32[256,4096]{1,0:T(8,128)} %orbitals.3, f32[2,4,2,16,1024]{4,3,2,1,0:T(8,128)S(1)} %bitcast.4, f32[3,128,128]{2,1,0:T(8,128)S(1)} %copy-done.5), custom_call_target="tpu_custom_call" | custom-call | tf_op jit(solution)/shard_map/exchange/pallas_call | solution.py:526
  163.6 0.0 copy-done.1
  163.6 0.0 copy-done.7
  163.6 0.0 copy-done.9
  163.6 0.0 copy-done.11
  163.6 0.0 copy-start.3
  163.6 2.2 %copy-done.3 = f32[256,4096]{1,0:T(8,128)S(1)} copy-done((f32[256,4096]{1,0:T(8,128)S(1)}, f32[256,4096]{1,0:T(8,128)}, u32[]{:S(2)}) %copy-start.3) | copy-done | bytes 4194328
  165.8 13.6 %update.1 = f32[256,4096]{1,0:T(8,128)} custom-call(s32[1]{0:T(128)} %bitcast.dom, s32[32]{0:T(128)S(1)} %copy-done.9, s32[32,32]{1,0:T(8,128)S(1)} %copy-done.7, s32[96]{0:T(128)S(1)} %copy-done.11, f32[96,256,128]{2,1,0:T(8,128)} %bitcast.5, f32[96,256,128]{2,1,0:T(8,128)} %bitcast.6, f32[96,256,128]{2,1,0:T(8,128)} %bitcast.7, f32[96,256,128]{2,1,0:T(8,128)} %bitcast.8, ...), custom_call_target="tpu_custom_call" | custom-call | flops 3221225472 | bytes 20971520 | tf_op jit(solution)/shard_map/update/pallas_call | solution.py:136
Async XLA Ops:
  0.0 3.4 %copy-start = (f32[32,512,128]{2,1,0:T(8,128)S(1)}, f32[32,512,128]{2,1,0:T(8,128)}, u32[]{:S(2)}) copy-start(f32[32,512,128]{2,1,0:T(8,128)} %refs_4_.1) | copy-start | bytes 25165828
  3.4 2.2 %copy-start.2 = (f32[256,4096]{1,0:T(8,128)S(1)}, f32[256,4096]{1,0:T(8,128)}, u32[]{:S(2)}) copy-start(f32[256,4096]{1,0:T(8,128)} %orbitals.3) | copy-start | bytes 12582916
  5.6 0.7 copy-start.6
  6.3 0.7 copy-start.8
  6.9 0.7 copy-start.10
  7.6 14.9 %copy-start.4 = (f32[256,1024]{1,0:T(8,128)S(1)}, f32[256,1024]{1,0:T(8,128)}, u32[]{:S(2)}) copy-start(f32[256,1024]{1,0:T(8,128)} %param.13) | copy-start | bytes 3145732
  7.6 14.9 %copy-start.5 = (f32[3,128,128]{2,1,0:T(8,128)S(1)}, f32[3,128,128]{2,1,0:T(8,128)}, u32[]{:S(2)}) copy-start(f32[3,128,128]{2,1,0:T(8,128)} %matrices.1) | copy-start | bytes 589828
  22.5 141.1 %copy-start.1 = (f32[32,512,128]{2,1,0:T(8,128)S(1)}, f32[32,512,128]{2,1,0:T(8,128)}, u32[]{:S(2)}) copy-start(f32[32,512,128]{2,1,0:T(8,128)} %refs_4_.1) | copy-start | bytes 25165828
  22.5 141.1 %copy-start.7 = (s32[32,32]{1,0:T(8,128)S(1)}, s32[32,32]{1,0:T(8,128)}, u32[]{:S(2)}) copy-start(s32[32,32]{1,0:T(8,128)} %slot_atom.3) | copy-start | bytes 12292
  22.5 141.1 %copy-start.9 = (s32[32]{0:T(128)S(1)}, s32[32]{0:T(128)}, u32[]{:S(2)}) copy-start(s32[32]{0:T(128)} %start.3) | copy-start | bytes 388
  22.5 141.1 %copy-start.11 = (s32[96]{0:T(128)S(1)}, s32[96]{0:T(128)}, u32[]{:S(2)}) copy-start(s32[96]{0:T(128)} %home.3) | copy-start | bytes 1156
  163.6 2.2 %copy-start.3 = (f32[256,4096]{1,0:T(8,128)S(1)}, f32[256,4096]{1,0:T(8,128)}, u32[]{:S(2)}) copy-start(f32[256,4096]{1,0:T(8,128)} %get-tuple-element.8.refs_5_) | copy-start | bytes 12582916

commit v3 on v2

v3 whole, which is shorter than its diff:
```python
import functools

import jax
import jax.numpy as jnp
from jax import lax
from jax.experimental import pallas as pl
from jax.experimental.pallas import tpu as pltpu
from jax.sharding import PartitionSpec as P

LANES = 128
GROUP = 4


def split(value):
    high = value.astype(jnp.bfloat16)
    low = (value - high.astype(jnp.float32)).astype(jnp.bfloat16)
    return high, low


def dot(a, b):
    return jnp.dot(a, b, preferred_element_type=jnp.float32)


def dot_nt(a, b):
    return lax.dot_general(a, b, (((1,), (1,)), ((), ())), preferred_element_type=jnp.float32)


def shifted(projector, pad, shift, window, wide):
    pad[pl.ds(LANES, window), :] = projector
    return split(pad[pl.ds(LANES - shift, wide), :])


def clear(pad, window):
    edge = jnp.zeros((LANES, pad.shape[1]), jnp.float32)
    pad[pl.ds(0, LANES), :] = edge
    pad[pl.ds(LANES + window, LANES), :] = edge


TILE, SHIFT, ROW, WHERE = 0, 1, 2, 3
TABLE_ROWS = 16


def list_kernel(dom, start, slot_atom, home, table, weights, *, group, cells, wide):
    lane = lax.broadcasted_iota(jnp.int32, (1, LANES), 1)
    blank = jnp.zeros((1, LANES), jnp.int32)
    none = jnp.full((1, LANES), -1, jnp.int32)
    core = lax.rem(dom[0], 2)

    def enter(domain):
        def body(slot, carry):
            row_of, where0, local0, where1, local1 = carry
            row = home[slot_atom[domain, slot]]
            owner = row // group
            local = row - owner * group
            here = lane == owner
            taken = here & (local0 >= 0)
            fresh = here & (local0 < 0)
            where1 = jnp.where(taken, slot, where1)
            local1 = jnp.where(taken, local, local1)
            where0 = jnp.where(fresh, slot, where0)
            local0 = jnp.where(fresh, local, local0)
            return jnp.where(lane == slot, row, row_of), where0, local0, where1, local1

        return lax.fori_loop(0, start.shape[0], body, (blank, blank, none, blank, none))

    def locate(slot, carry):
        tile = jnp.minimum(start[slot] // LANES, (cells - wide) // LANES)
        cell_of, shift_of = carry
        cell_of = jnp.where(lane == slot, tile, cell_of)
        return cell_of, jnp.where(lane == slot, start[slot] - tile * LANES, shift_of)

    cell_of, shift_of = lax.fori_loop(0, start.shape[0], locate, (blank, blank))
    row_of, own0, own_local0, own1, own_local1 = enter(dom[0])
    _, mate0, mate_local0, mate1, mate_local1 = enter(dom[0] + 1 - 2 * core)
    rows = [cell_of, shift_of, row_of, own0, own1, mate0, mate1]
    for index, row in enumerate(rows):
        table[index : index + 1, :] = row
    for index, local in enumerate([own_local0, own_local1, mate_local0, mate_local1]):
        for atom in range(group):
            at = index * group + atom
            weights[at : at + 1, :] = (local == atom).astype(jnp.float32)


def list_slots(dom, start, slot_atom, home, group, cells, wide):
    return pl.pallas_call(
        functools.partial(list_kernel, group=group, cells=cells, wide=wide),
        out_shape=[jax.ShapeDtypeStruct((TABLE_ROWS, LANES), kind) for kind in (jnp.int32, jnp.float32)],
        in_specs=[pl.BlockSpec(memory_space=pltpu.SMEM)] * 4,
        out_specs=[pl.BlockSpec(memory_space=pltpu.VMEM)] * 2,
        compiler_params=pltpu.CompilerParams(vmem_limit_bytes=60 << 20),
        name="list_slots",
    )(dom, start, slot_atom, home)


def update_kernel(table, *refs):
    group = GROUP
    factors = refs[:group]
    projectors, rotated, out = refs[group : group + 3]
    pads = refs[group + 3 : -1]
    step = pl.program_id(0)
    fetch = pltpu.make_async_copy(rotated, out, refs[-1])
    _, window, _ = projectors.shape
    cells = out.shape[1]
    wide = window + LANES

    @pl.when(step == 0)
    def _():
        fetch.start()
        for pad in pads:
            clear(pad, window)
        fetch.wait()

    for k in range(group):
        slot = step * group + k
        cell, shift = pl.multiple_of(table[TILE, slot] * LANES, LANES), table[SHIFT, slot]
        p_high, p_low = shifted(projectors[k], pads[k], shift, window, wide)
        f_high, f_low = split(factors[k][0])
        update = dot_nt(
            jnp.concatenate([f_high, f_low, f_high], axis=1),
            jnp.concatenate([p_high, p_high, p_low], axis=1),
        )
        out[:, pl.ds(cell, wide)] += update


def update(table, factors, projectors, rotated):
    slots, window, projs = projectors.shape
    bands, cells = rotated.shape

    def factor_spec(k):
        return pl.BlockSpec(
            (1, bands, projs),
            lambda i, table: (table[ROW, i * GROUP + k], 0, 0),
        )

    return pl.pallas_call(
        update_kernel,
        out_shape=jax.ShapeDtypeStruct((bands, cells), jnp.float32),
        grid_spec=pltpu.PrefetchScalarGridSpec(
            num_scalar_prefetch=1,
            grid=(slots // GROUP,),
            in_specs=[factor_spec(k) for k in range(GROUP)]
            + [
                pl.BlockSpec((GROUP, window, projs), lambda i, *_: (i, 0, 0)),
                pl.BlockSpec(memory_space=pltpu.MemorySpace.HBM),
            ],
            out_specs=pl.BlockSpec(
                (bands, cells), lambda i, *_: (0, 0), pipeline_mode=pl.Buffered(1)
            ),
            scratch_shapes=[pltpu.VMEM((window + 2 * LANES, projs), jnp.float32)] * GROUP
            + [pltpu.SemaphoreType.DMA],
        ),
        cost_estimate=pl.CostEstimate(
            flops=6 * slots * window * bands * projs, bytes_accessed=20 << 20, transcendentals=0
        ),
        compiler_params=pltpu.CompilerParams(vmem_limit_bytes=60 << 20),
        name="update",
    )(table, *([factors] * GROUP), projectors, rotated)


MESH = pl.DeviceIdType.MESH
RING = 4
ORDER = (2, 1, 3, 0)


def ring(position, offset):
    return lax.rem(position + offset, RING)


def tile_of(index, size):
    return pl.ds(pl.multiple_of(index * size, size), size)


class Links:
    def __init__(self):
        self.band = lax.axis_index("band")
        dom = lax.axis_index("dom")
        self.core = lax.rem(dom, 2)
        self.z = lax.rem(dom // 2, RING)
        self.x = dom // (2 * RING)

    def place(self, band, x, z, core):
        return (band, (x * RING + z) * 2 + core)

    def at_band(self, offset):
        return self.place(ring(self.band, offset), self.x, self.z, self.core)

    def at_x(self, offset):
        return self.place(self.band, ring(self.x, offset), self.z, self.core)

    def at_z(self, offset):
        return self.place(self.band, self.x, ring(self.z, offset), self.core)

    def partner(self):
        return self.place(self.band, self.x, self.z, 1 - self.core)


def exchange_kernel(
    table, weights, orbitals, projectors, rotation, matrices, factors, rotated,
    cells_in, cells_out, full, high_rows, low_rows, high_cells, low_cells, tiles, windows, mate, total, hop1, hop2, hop3, hop4,
    turn, turn_in, turn_out, turned, owned, pads,
    sem_load, sem_keep, sem_own, *sems
):
    link = Links()
    b, x, z, c = link.band, link.x, link.z, link.core
    names = ("yin", "yout", "r1", "r2", "r3", "s0", "one", "two", "sum", "back", "ag1", "ag2", "agf", "core")
    send = dict(zip(names, sems[0::2]))
    recv = dict(zip(names, sems[1::2]))
    bands, cells = orbitals.shape
    slots, window, projs = projectors.shape
    wide = window + LANES
    group = matrices.shape[0]
    quarter = cells // RING
    parts = cells_in.shape[0]
    width = quarter // parts
    half = bands // 2
    sub = half // 2
    strip = turn.shape[0] // RING
    started = []

    def push(src, dst, kind, index, device):
        copy = pltpu.make_async_remote_copy(
            src_ref=src, dst_ref=dst, send_sem=send[kind].at[index], recv_sem=recv[kind].at[index],
            device_id=device, device_id_type=MESH,
        )
        copy.start()
        started.append(copy)
        return copy

    def keep(src, dst, sem):
        copy = pltpu.make_async_copy(src, dst, sem)
        copy.start()
        return copy

    barrier = pltpu.get_barrier_semaphore()
    peers = [f(o) for f in (link.at_band, link.at_x, link.at_z) for o in (1, 2, 3)] + [link.partner()]
    for peer in peers:
        pl.semaphore_signal(barrier, inc=1, device_id=peer, device_id_type=MESH)
    pl.semaphore_wait(barrier, len(peers))

    first = (x, z)
    second = (z, x)
    at_first = (link.at_x, link.at_z)
    at_second = (link.at_z, link.at_x)

    def factor_at(h, t, u, core, low=0, size=None):
        rows = pl.ds(h * half + low, half if size is None else size)
        if h == 0:
            return factors.at[t, u, core, :, rows, :]
        return factors.at[u, t, core, :, rows, :]

    stage = [keep(orbitals.at[:, tile_of(q, quarter)], cells_out.at[q], sem_load.at[q]) for q in range(RING)]
    eighth = slots // RING
    stage_tiles = [
        keep(projectors.at[pl.ds(q * eighth, eighth)], tiles.at[pl.ds(q * eighth, eighth)], sem_load.at[RING + q])
        for q in range(RING)
    ]
    r1 = {}
    for o in (1, 2, 3):
        for h in range(2):
            piece = (h, first[h], c)
            r1[o, h] = push(rotation.at[piece], full.at[(b,) + piece], "r1", (o - 1, h), link.at_band(o))
    own_rows = keep(rotation, full.at[b], sem_own.at[0])
    yin, own_cells = {}, []
    for i in range(parts):
        for o in (1, 2, 3):
            src = orbitals.at[:, tile_of(ring(b, o) * parts + i, width)]
            yin[i, o] = push(src, cells_in.at[i, b], "yin", (i, o - 1), link.at_band(o))
        own_cells.append(keep(orbitals.at[:, tile_of(b * parts + i, width)], cells_in.at[i, b], sem_keep.at[i]))

    for k in range(GROUP):
        clear(pads.at[k], window)
    for q in range(RING):
        stage[q].wait()
        top, rest = split(cells_out[q])
        for m in range(quarter // LANES):
            high_cells[q * (quarter // LANES) + m] = top[:, m * LANES : (m + 1) * LANES]
            low_cells[q * (quarter // LANES) + m] = rest[:, m * LANES : (m + 1) * LANES]
    for copy in stage_tiles:
        copy.wait()

    def to_mate(step):
        group_at = pl.ds(step * GROUP, GROUP)
        return pltpu.make_async_remote_copy(
            src_ref=windows.at[group_at], dst_ref=mate.at[group_at],
            send_sem=send["s0"].at[step], recv_sem=recv["s0"].at[step],
            device_id=link.partner(), device_id_type=MESH,
        )

    def take(step, carry):
        for k in range(GROUP):
            index = step * GROUP + k
            tile, shift = table[TILE, index], table[SHIFT, index]
            o_high, o_low = [
                jnp.concatenate([ref[tile + m] for m in range(wide // LANES)], axis=1) for ref in (high_cells, low_cells)
            ]
            p_high, p_low = shifted(tiles[index], pads.at[k], shift, window, wide)
            both = dot(o_high, jnp.concatenate([p_high, p_low], axis=1))
            windows[index] = both[:, :projs] + both[:, projs:] + dot(o_low, p_high)
        to_mate(step).start()
        return carry

    one, two = {}, {}

    def assemble(h, o):
        t = ring(first[h], o)
        rows = pl.ds(h * half, half)

        def body(u, carry):
            owner = (t * RING + u if h == 0 else u * RING + t) * 2 + c
            values = [
                ref[table[WHERE + k, owner], rows, :] for k, ref in enumerate((windows, windows, mate, mate))
            ]
            for atom in range(group):
                a, d, e, f = [value * weights[k * group + atom, owner] for k, value in enumerate(values)]
                total[h, t, u, atom] = (a + d) + (e + f)
            return carry

        lax.fori_loop(0, RING, body, 0)
        return t

    low2, high2 = pl.ds(0, 2), pl.ds(2, 2)

    def send_far(h):
        t = assemble(h, 2)
        one[h, 0, 0] = push(total.at[h, t, low2], hop1.at[h, 0], "one", (h, 0, 0), at_first[h](1))
        one[h, 1, 0] = push(total.at[h, t, high2], hop1.at[h, 1], "one", (h, 1, 0), at_first[h](3))

    steps = slots // GROUP
    lax.fori_loop(0, steps // 4, take, 0)

    r2 = {}
    for o in (1, 2, 3):
        k = ring(b, RING - o)
        for h in range(2):
            r1[o, h].wait_recv()
            piece = (k, h, first[h], c)
            for p in (1, 2, 3):
                r2[o, p, h] = push(full.at[piece], full.at[piece], "r2", (o - 1, p - 1, h), at_first[h](p))

    lax.fori_loop(steps // 4, steps, take, 0)
    for step in range(steps):
        to_mate(step).wait_recv()
    for h in range(2):
        send_far(h)
    for h in range(2):
        t = assemble(h, 1)
        one[h, 0, 1] = push(total.at[h, t, high2], hop2.at[h, 0, high2], "one", (h, 0, 1), at_first[h](1))
    for h in range(2):
        t = assemble(h, 3)
        one[h, 1, 1] = push(total.at[h, t, low2], hop2.at[h, 1, low2], "one", (h, 1, 1), at_first[h](3))
    for h in range(2):
        assemble(h, 0)

    def add_rows(h, t, start, source):
        def body(u, carry):
            total[h, t, start + u] += source[h, start // 2, u]
            return carry

        lax.fori_loop(0, 2, body, 0)

    for h in range(2):
        one[h, 0, 0].wait_recv()
        t = ring(first[h], 1)
        add_rows(h, t, 0, hop1)
        one[h, 0, 2] = push(total.at[h, t, low2], hop2.at[h, 0, low2], "one", (h, 0, 2), at_first[h](1))
        one[h, 1, 0].wait_recv()
        t = ring(first[h], 3)
        add_rows(h, t, 2, hop1)
        one[h, 1, 2] = push(total.at[h, t, high2], hop2.at[h, 1, high2], "one", (h, 1, 2), at_first[h](3))

    r3 = {}
    for o in (1, 2, 3):
        k = ring(b, RING - o)
        for h in range(2):
            for p in (1, 2, 3):
                r2[o, p, h].wait_recv()
        mine = full.at[k, :, :, c]
        r3[o] = push(mine, mine, "r3", (o - 1,), link.partner())

    own_rows.wait()
    for o in (1, 2, 3):
        r3[o].wait_recv()

    def split_rows(k, carry):
        top, rest = split(full[k].reshape(bands, full.shape[-1]))
        columns = tile_of(k, full.shape[-1])
        high_rows[:, columns] = top
        low_rows[:, columns] = rest
        return carry

    lax.fori_loop(0, RING, split_rows, 0)

    yout, own_out = {}, []

    def rotate(i):
        for o in (1, 2, 3):
            yin[i, o].wait_recv()
        own_cells[i].wait()
        high, low = split(cells_in[i].reshape(RING * bands, width))
        pair = jnp.concatenate([high, low], axis=1)

        def body(k, carry):
            columns = tile_of(k, full.shape[-1])
            both = dot(high_rows[:, columns], pair)
            here = both[:, :width] + both[:, width:] + dot(low_rows[:, columns], high)
            cells_out[k, :, pl.ds(i * width, width)] = here
            return carry

        lax.fori_loop(0, RING, body, 0)
    def give(i):
        columns = tile_of(b * parts + i, width)
        for o in (1, 2, 3):
            src = cells_out.at[ring(b, o), :, pl.ds(i * width, width)]
            yout[i, o] = push(src, rotated.at[:, columns], "yout", (i, o - 1), link.at_band(o))
        own_out.append(keep(cells_out.at[b, :, pl.ds(i * width, width)], rotated.at[:, columns], sem_keep.at[parts + i]))

    for i in range(parts // 2):
        rotate(i)
    give(0)

    for h in range(2):
        t = first[h]
        one[h, 0, 1].wait_recv()
        one[h, 1, 1].wait_recv()
        one[h, 0, 2].wait_recv()
        one[h, 1, 2].wait_recv()

        def finish(u, carry, h=h, t=t):
            total[h, t, u] += hop2[h, 0, u] + hop2[h, 1, u]
            return carry

        lax.fori_loop(0, RING, finish, 0)
        lower, upper = pl.ds(0, sub), pl.ds(sub, sub)
        s = second[h]
        far, nxt, prv = ring(s, 2), ring(s, 1), ring(s, 3)
        two[h, 0, 0] = push(total.at[h, t, far, :, lower], hop3.at[h, 0], "two", (h, 0, 0), at_second[h](1))
        two[h, 1, 0] = push(total.at[h, t, far, :, upper], hop3.at[h, 1], "two", (h, 1, 0), at_second[h](3))
        two[h, 0, 1] = push(
            total.at[h, t, nxt, :, upper], hop4.at[h, 0, :, upper], "two", (h, 0, 1), at_second[h](1)
        )
        two[h, 1, 1] = push(
            total.at[h, t, prv, :, lower], hop4.at[h, 1, :, lower], "two", (h, 1, 1), at_second[h](3)
        )

    for h in range(2):
        t, s = first[h], second[h]
        nxt, prv = ring(s, 1), ring(s, 3)
        two[h, 0, 0].wait_recv()
        total[h, t, nxt, :, lower] += hop3[h, 0]
        two[h, 0, 2] = push(
            total.at[h, t, nxt, :, lower], hop4.at[h, 0, :, lower], "two", (h, 0, 2), at_second[h](1)
        )
        two[h, 1, 0].wait_recv()
        total[h, t, prv, :, upper] += hop3[h, 1]
        two[h, 1, 2] = push(
            total.at[h, t, prv, :, upper], hop4.at[h, 1, :, upper], "two", (h, 1, 2), at_second[h](3)
        )

    rotate(parts // 2)
    rotate(parts // 2 + 1)

    for h in range(2):
        t, s = first[h], second[h]
        for d in range(2):
            two[h, d, 1].wait_recv()
            two[h, d, 2].wait_recv()
        for atom in range(group):
            value = total[h, t, s, atom] + hop4[h, 0, atom] + hop4[h, 1, atom]
            turn[pl.ds(atom * projs, projs), pl.ds(h * half, half)] = value.T

    def strip_at(index):
        return pl.ds(pl.multiple_of(index * strip, 8), strip)

    swap, back = {}, {}
    for o in (1, 2, 3):
        swap[o] = push(turn.at[strip_at(ring(b, o))], turn_in.at[b], "sum", (o - 1,), link.at_band(o))
    turn_in[b] = turn[strip_at(b), :]
    give(1)

    for o in (1, 2, 3):
        swap[o].wait_recv()
    high, low = split(jnp.concatenate([turn_in[k] for k in range(RING)], axis=1))
    pair = jnp.concatenate([high, low], axis=0)

    def turn_rows(k, carry):
        columns = tile_of(k, full.shape[-1])
        both = dot_nt(pair, high_rows[:, columns])
        turn_out[k] = both[:strip] + both[strip:] + dot_nt(high, low_rows[:, columns])
        return carry

    lax.fori_loop(0, RING, turn_rows, 0)
    for o in (1, 2, 3):
        back[o] = push(turn_out.at[ring(b, o)], turned.at[strip_at(b)], "back", (o - 1,), link.at_band(o))
    turned[strip_at(b), :] = turn_out[b]

    for i in range(2, parts // 2 + 2):
        give(i)
    for i in range(parts // 2 + 2, parts):
        rotate(i)
        give(i)

    for o in (1, 2, 3):
        back[o].wait_recv()
    for atom in range(group):
        t_high, t_low = split(turned[pl.ds(atom * projs, projs), :].T)
        m_high, m_low = split(matrices[atom])
        both = dot(t_high, jnp.concatenate([m_high, m_low], axis=1))
        owned[atom] = both[:, :projs] + both[:, projs:] + dot(t_low, m_high)

    own_factor = keep(owned, factors.at[x, z, c], sem_own.at[1])
    mate_core = []

    def to_core(src, h, t, u, index):
        mate_core.append(push(src, factor_at(h, t, u, c), "core", (h, index), link.partner()))

    ag1, ag2, agf = {}, {}, {}
    for h in range(2):
        t, s = first[h], second[h]
        for d, peer, order in ((0, 1, (0, 1)), (1, 3, (1, 0))):
            for m, part in enumerate(order):
                rows = pl.ds(h * half + part * sub, sub)
                ag1[h, d, m] = push(
                    owned.at[:, rows], factor_at(h, t, s, c, part * sub, sub), "ag1", (h, d, m), at_second[h](peer)
                )
    def spread(h, r, src, u):
        t = first[h]
        for d, peer in ((0, 1), (1, 3)):
            ag2[h, d, r] = push(src, factor_at(h, t, u, c), "ag2", (h, d, r), at_first[h](peer))
        to_core(src, h, t, u, r)

    lines = (0, 3, 1, 2)
    for h in range(2):
        spread(h, 0, owned.at[:, pl.ds(h * half, half)], second[h])
    for h in range(2):
        t, s = first[h], second[h]
        for d, back, peer in ((0, 3, 1), (1, 1, 3)):
            ag1[h, d, 0].wait_recv()
            piece = factor_at(h, t, ring(s, back), c, d * sub, sub)
            ag1[h, d, 2] = push(piece, piece, "ag1", (h, d, 2), at_second[h](peer))
    for h in range(2):
        t, s = first[h], second[h]
        for d, r in ((0, 1), (1, 2)):
            ag1[h, d, 1].wait_recv()
            u = ring(s, lines[r])
            spread(h, r, factor_at(h, t, u, c), u)
    for h in range(2):
        t, s = first[h], second[h]
        ag1[h, 0, 2].wait_recv()
        ag1[h, 1, 2].wait_recv()
        u = ring(s, 2)
        spread(h, 3, factor_at(h, t, u, c), u)

    for r in range(RING):
        for h in range(2):
            u = ring(second[h], lines[r])
            for d, back, peer in ((0, 3, 1), (1, 1, 3)):
                ag2[h, d, r].wait_recv()
                t = ring(first[h], back)
                piece = factor_at(h, t, u, c)
                if (r < 2) == (d == 0):
                    agf[h, r] = push(piece, piece, "agf", (h, r), at_first[h](peer))
                to_core(piece, h, t, u, RING * (1 + d) + r)
    for r in range(RING):
        for h in range(2):
            u = ring(second[h], lines[r])
            agf[h, r].wait_recv()
            t = ring(first[h], 2)
            to_core(factor_at(h, t, u, c), h, t, u, RING * 3 + r)

    for copy in mate_core:
        copy.wait_recv()
    for copy in yout.values():
        copy.wait_recv()
    for copy in own_out:
        copy.wait()
    own_factor.wait()
    for copy in started:
        copy.wait_send()
    for step in range(slots // GROUP):
        to_mate(step).wait_send()


PARTS = 8


def exchange(table, weights, orbitals, projectors, rotation, matrices):
    bands, cells = orbitals.shape
    slots, window, projs = projectors.shape
    all_bands = rotation.shape[1]
    group = matrices.shape[0]
    atoms = 2 * RING * RING * group
    width = cells // RING // PARTS
    half = bands // 2
    sub = half // 2
    rows = bands // (4 * RING)
    strip = group * projs // RING
    f32, bf16 = jnp.float32, jnp.bfloat16
    counts = [
        (PARTS, 3), (PARTS, 3), (3, 2), (3, 3, 2), (3,), (slots // GROUP,), (2, 2, 3), (2, 2, 3), (3,), (3,),
        (2, 2, 3), (2, 2, RING), (2, RING), (2, 4 * RING),
    ]
    dma = pltpu.SemaphoreType.DMA
    in_hbm = pl.BlockSpec(memory_space=pltpu.MemorySpace.HBM)
    factors, rotated = pl.pallas_call(
        exchange_kernel,
        out_shape=(
            jax.ShapeDtypeStruct((RING, RING, 2, group, bands, projs), f32),
            jax.ShapeDtypeStruct((bands, cells), f32),
        ),
        in_specs=[pl.BlockSpec(memory_space=pltpu.SMEM)] * 2
        + [in_hbm] * 3
        + [pl.BlockSpec(memory_space=pltpu.VMEM)],
        out_specs=[in_hbm] * 2,
        scratch_shapes=[
            pltpu.VMEM((PARTS, RING, bands, width), f32),
            pltpu.VMEM((RING, bands, cells // RING), f32),
            pltpu.VMEM((RING, 2, RING, 2, rows, all_bands), f32),
            pltpu.VMEM((bands, RING * all_bands), bf16),
            pltpu.VMEM((bands, RING * all_bands), bf16),
            pltpu.VMEM((cells // LANES, bands, LANES), bf16),
            pltpu.VMEM((cells // LANES, bands, LANES), bf16),
            pltpu.VMEM((slots, window, projs), f32),
            pltpu.VMEM((slots, bands, projs), f32),
            pltpu.VMEM((slots, bands, projs), f32),
            pltpu.VMEM((2, RING, RING, group, half, projs), f32),
            pltpu.VMEM((2, 2, 2, group, half, projs), f32),
            pltpu.VMEM((2, 2, RING, group, half, projs), f32),
            pltpu.VMEM((2, 2, group, sub, projs), f32),
            pltpu.VMEM((2, 2, group, half, projs), f32),
            pltpu.VMEM((group * projs, bands), f32),
            pltpu.VMEM((RING, strip, bands), f32),
            pltpu.VMEM((RING, strip, bands), f32),
            pltpu.VMEM((group * projs, bands), f32),
            pltpu.VMEM((group, bands, projs), f32),
            pltpu.VMEM((GROUP, window + 2 * LANES, projs), f32),
            dma((2 * RING,)),
            dma((2 * PARTS,)),
            dma((2,)),
        ]
        + [dma(shape) for shape in counts for _ in range(2)],
        compiler_params=pltpu.CompilerParams(
            collective_id=0, has_side_effects=True, vmem_limit_bytes=60 << 20
        ),
        name="exchange",
    )(
        table, weights, orbitals, projectors, rotation.reshape(2, RING, 2, rows, all_bands), matrices
    )
    return factors.reshape(atoms, bands, projs), rotated


def per_device(orbitals, projectors, window_start, slot_atom, atom_home, atom_matrices, rotation):
    dom = lax.axis_index("dom").astype(jnp.int32).reshape(1)
    window = projectors.shape[1]
    table, weights = list_slots(
        dom, window_start, slot_atom, atom_home, atom_matrices.shape[0], orbitals.shape[1], window + LANES
    )
    factors, rotated = exchange(table, weights, orbitals, projectors, rotation, atom_matrices)
    return update(table, factors, projectors, rotated)


def solution(mesh):
    in_specs = (
        P("band", "dom"),
        P("dom", None, None),
        P("dom"),
        P(),
        P(),
        P("dom", None, None),
        P("band", None),
    )
    out_specs = P("band", "dom")
    return jax.shard_map(
        per_device, mesh=mesh, in_specs=in_specs, out_specs=out_specs, check_vma=False
    )
```

time: 180 us -> 142 us (0.79)
  Pallas kernels: 170 us -> 142 us
  local copies, waits for them, and re-layouts: 9.8 us -> 0 us
    pallas_call x1, Pallas kernels: 141 us -> 121 us  [exchange(): pl.pallas_call(exchange_kernel, out_shape=(jax.ShapeDtypeStruct((RING, RI...]
    pallas_call x1, Pallas kernels: 14.8 us -> 3.42 us  [list_slots(): pl.pallas_call(functools.partial(list_kernel, group=group, cells=cells, w...]
    unnamed x24 -> x0, local copies, waits for them, and re-layouts: 9.8 us -> none
    pallas_call x1, Pallas kernels: 13.6 us -> 16.7 us  [update(): pl.pallas_call(update_kernel, out_shape=jax.ShapeDtypeStruct((bands, cell...]
where the time goes in v3:
time: 142 us
  Pallas kernels  142 us (100%)
    pallas_call x1, Pallas kernels, exchange(): pl.pallas_call(exchange_kernel, out_shape=(jax.ShapeDtypeStruct((RING, RI...  121 us
    pallas_call x1, Pallas kernels, update(): pl.pallas_call(update_kernel, out_shape=jax.ShapeDtypeStruct((bands, cell...  16.7 us
    pallas_call x1, Pallas kernels, list_slots(): pl.pallas_call(functools.partial(list_kernel, group=group, cells=cells, w...  3.42 us

profile of v3, /device:TPU:1, one launch (start us, length us, event | category | flops | bytes accessed | tf_op | source)
XLA Modules:
  0.0 141.6 jit_solution(11809107584374858748)
XLA Ops:
  0.0 3.4 %list_slots.1 = (s32[16,128]{1,0:T(8,128)}, f32[16,128]{1,0:T(8,128)}) custom-call(s32[1]{0:T(128)} %bitcast.dom, s32[32]{0:T(128)} %start.1, s32[32,32]{1,0:T(8,128)} %slot_atom.1, s32[96]{0:T(128)} %home.1), custom_call_target="tpu_custom_call" | custom-call | tf_op jit(solution)/shard_map/list_slots/pallas_call | solution.py:85
  3.4 121.5 %exchange.1 = (f32[4,4,2,3,256,128]{5,4,3,2,1,0:T(8,128)}, f32[256,4096]{1,0:T(8,128)}) custom-call(s32[16,128]{1,0:T(8,128)} %get-tuple-element.9.table, f32[16,128]{1,0:T(8,128)} %get-tuple-element.10.weights, f32[256,4096]{1,0:T(8,128)} %orbitals.1, f32[32,512,128]{2,1,0:T(8,128)} %refs_4_.1, f32[2,4,2,16,1024]{4,3,2,1,0:T(8,128)} %bitcast.7, ...), custom_call_target="tpu_custom_call" | custom-call | tf_op jit(solution)/shard_map/exchange/pallas_call | solution.py:604
  124.9 16.7 %update.1 = f32[256,4096]{1,0:T(8,128)} custom-call(s32[16,128]{1,0:T(8,128)} %get-tuple-element.9.table, f32[96,256,128]{2,1,0:T(8,128)} %bitcast.3, f32[96,256,128]{2,1,0:T(8,128)} %bitcast.4, f32[96,256,128]{2,1,0:T(8,128)} %bitcast.5, f32[96,256,128]{2,1,0:T(8,128)} %bitcast.6, f32[32,512,128]{2,1,0:T(8,128)} %refs_4_.1, ...), custom_call_target="tpu_custom_call" | custom-call | flops 3221225472 | bytes 20971520 | tf_op jit(solution)/shard_map/update/pallas_call | solution.py:135

commit v4 on v3

--- a/solution.py
+++ b/solution.py
@@ -9,6 +9,7 @@
 
 LANES = 128
 GROUP = 4
+UPDATE_GROUP = 8
 
 
 def split(value):
@@ -61,7 +62,7 @@
             local0 = jnp.where(fresh, local, local0)
             return jnp.where(lane == slot, row, row_of), where0, local0, where1, local1
 
-        return lax.fori_loop(0, start.shape[0], body, (blank, blank, none, blank, none))
+        return lax.fori_loop(0, start.shape[0], body, (blank, blank, none, blank, none), unroll=8)
 
     def locate(slot, carry):
         tile = jnp.minimum(start[slot] // LANES, (cells - wide) // LANES)
@@ -69,7 +70,7 @@
         cell_of = jnp.where(lane == slot, tile, cell_of)
         return cell_of, jnp.where(lane == slot, start[slot] - tile * LANES, shift_of)
 
-    cell_of, shift_of = lax.fori_loop(0, start.shape[0], locate, (blank, blank))
+    cell_of, shift_of = lax.fori_loop(0, start.shape[0], locate, (blank, blank), unroll=8)
     row_of, own0, own_local0, own1, own_local1 = enter(dom[0])
     _, mate0, mate_local0, mate1, mate_local1 = enter(dom[0] + 1 - 2 * core)
     rows = [cell_of, shift_of, row_of, own0, own1, mate0, mate1]
@@ -93,12 +94,12 @@
 
 
 def update_kernel(table, *refs):
-    group = GROUP
+    group = UPDATE_GROUP
     factors = refs[:group]
     projectors, rotated, out = refs[group : group + 3]
-    pads = refs[group + 3 : -1]
+    pads, base = refs[group + 3 : -2], refs[-2]
     step = pl.program_id(0)
-    fetch = pltpu.make_async_copy(rotated, out, refs[-1])
+    fetch = pltpu.make_async_copy(rotated, base, refs[-1])
     _, window, _ = projectors.shape
     cells = out.shape[1]
     wide = window + LANES
@@ -108,7 +109,7 @@
         fetch.start()
         for pad in pads:
             clear(pad, window)
-        fetch.wait()
+        out[...] = jnp.zeros_like(out)
 
     for k in range(group):
         slot = step * group + k
@@ -121,6 +122,11 @@
         )
         out[:, pl.ds(cell, wide)] += update
 
+    @pl.when(step == pl.num_programs(0) - 1)
+    def _():
+        fetch.wait()
+        out[...] += base[...]
+
 
 def update(table, factors, projectors, rotated):
     slots, window, projs = projectors.shape
@@ -129,7 +135,7 @@
     def factor_spec(k):
         return pl.BlockSpec(
             (1, bands, projs),
-            lambda i, table: (table[ROW, i * GROUP + k], 0, 0),
+            lambda i, table: (table[ROW, i * UPDATE_GROUP + k], 0, 0),
         )
 
     return pl.pallas_call(
@@ -137,24 +143,24 @@
         out_shape=jax.ShapeDtypeStruct((bands, cells), jnp.float32),
         grid_spec=pltpu.PrefetchScalarGridSpec(
             num_scalar_prefetch=1,
-            grid=(slots // GROUP,),
-            in_specs=[factor_spec(k) for k in range(GROUP)]
+            grid=(slots // UPDATE_GROUP,),
+            in_specs=[factor_spec(k) for k in range(UPDATE_GROUP)]
             + [
-                pl.BlockSpec((GROUP, window, projs), lambda i, *_: (i, 0, 0)),
+                pl.BlockSpec((UPDATE_GROUP, window, projs), lambda i, *_: (i, 0, 0)),
                 pl.BlockSpec(memory_space=pltpu.MemorySpace.HBM),
             ],
             out_specs=pl.BlockSpec(
                 (bands, cells), lambda i, *_: (0, 0), pipeline_mode=pl.Buffered(1)
             ),
-            scratch_shapes=[pltpu.VMEM((window + 2 * LANES, projs), jnp.float32)] * GROUP
-            + [pltpu.SemaphoreType.DMA],
+            scratch_shapes=[pltpu.VMEM((window + 2 * LANES, projs), jnp.float32)] * UPDATE_GROUP
+            + [pltpu.VMEM((bands, cells), jnp.float32), pltpu.SemaphoreType.DMA],
         ),
         cost_estimate=pl.CostEstimate(
             flops=6 * slots * window * bands * projs, bytes_accessed=20 << 20, transcendentals=0
         ),
         compiler_params=pltpu.CompilerParams(vmem_limit_bytes=60 << 20),
         name="update",
-    )(table, *([factors] * GROUP), projectors, rotated)
+    )(table, *([factors] * UPDATE_GROUP), projectors, rotated)
 
 
 MESH = pl.DeviceIdType.MESH
@@ -202,7 +208,7 @@
 ):
     link = Links()
     b, x, z, c = link.band, link.x, link.z, link.core
-    names = ("yin", "yout", "r1", "r2", "r3", "s0", "one", "two", "sum", "back", "ag1", "ag2", "agf", "core")
+    names = ("yin", "yout", "r1", "r2", "r3", "r4", "s0", "one", "two", "sum", "back", "ag1", "ag2", "agf", "core")
     send = dict(zip(names, sems[0::2]))
     recv = dict(zip(names, sems[1::2]))
     bands, cells = orbitals.shape
@@ -256,9 +262,7 @@
     ]
     r1 = {}
     for o in (1, 2, 3):
-        for h in range(2):
-            piece = (h, first[h], c)
-            r1[o, h] = push(rotation.at[piece], full.at[(b,) + piece], "r1", (o - 1, h), link.at_band(o))
+        r1[o] = push(rotation.at[x, z, c], full.at[b, x, z, c], "r1", (o - 1,), link.at_band(o))
     own_rows = keep(rotation, full.at[b], sem_own.at[0])
     yin, own_cells = {}, []
     for i in range(parts):
@@ -269,14 +273,31 @@
 
     for k in range(GROUP):
         clear(pads.at[k], window)
+    r2, r3, r4 = {}, {}, {}
+    columns_of = [pl.ds(h * (full.shape[-1] // 2), full.shape[-1] // 2) for h in range(2)]
+    for o in (1, 2, 3):
+        r1[o].wait_recv()
+        for h in range(2):
+            piece = full.at[ring(b, RING - o), x, z, c, :, columns_of[h]]
+            for p in (1, 2, 3):
+                r2[o, p, h] = push(piece, piece, "r2", (o - 1, p - 1, h), at_first[h](p))
     for q in range(RING):
         stage[q].wait()
         top, rest = split(cells_out[q])
         for m in range(quarter // LANES):
             high_cells[q * (quarter // LANES) + m] = top[:, m * LANES : (m + 1) * LANES]
             low_cells[q * (quarter // LANES) + m] = rest[:, m * LANES : (m + 1) * LANES]
-    for copy in stage_tiles:
-        copy.wait()
+    for o in (1, 2, 3):
+        k = ring(b, RING - o)
+        for h in range(2):
+            for p in (1, 2, 3):
+                r2[o, p, h].wait_recv()
+            if h == 0:
+                piece = full.at[k, :, z, c, :, columns_of[h]]
+            else:
+                piece = full.at[k, x, :, c, :, columns_of[h]]
+            for p in (1, 2, 3):
+                r3[o, p, h] = push(piece, piece, "r3", (o - 1, p - 1, h), at_second[h](p))
 
     def to_mate(step):
         group_at = pl.ds(step * GROUP, GROUP)
@@ -326,18 +347,9 @@
         one[h, 1, 0] = push(total.at[h, t, high2], hop1.at[h, 1], "one", (h, 1, 0), at_first[h](3))
 
     steps = slots // GROUP
-    lax.fori_loop(0, steps // 4, take, 0)
-
-    r2 = {}
-    for o in (1, 2, 3):
-        k = ring(b, RING - o)
-        for h in range(2):
-            r1[o, h].wait_recv()
-            piece = (k, h, first[h], c)
-            for p in (1, 2, 3):
-                r2[o, p, h] = push(full.at[piece], full.at[piece], "r2", (o - 1, p - 1, h), at_first[h](p))
-
-    lax.fori_loop(steps // 4, steps, take, 0)
+    for q in range(RING):
+        stage_tiles[q].wait()
+        lax.fori_loop(q * steps // RING, (q + 1) * steps // RING, take, 0)
     for step in range(steps):
         to_mate(step).wait_recv()
     for h in range(2):
@@ -368,18 +380,16 @@
         add_rows(h, t, 2, hop1)
         one[h, 1, 2] = push(total.at[h, t, high2], hop2.at[h, 1, high2], "one", (h, 1, 2), at_first[h](3))
 
-    r3 = {}
-    for o in (1, 2, 3):
-        k = ring(b, RING - o)
+    for o in (1, 2, 3):
         for h in range(2):
             for p in (1, 2, 3):
-                r2[o, p, h].wait_recv()
-        mine = full.at[k, :, :, c]
-        r3[o] = push(mine, mine, "r3", (o - 1,), link.partner())
+                r3[o, p, h].wait_recv()
+        mine = full.at[ring(b, RING - o), :, :, c]
+        r4[o] = push(mine, mine, "r4", (o - 1,), link.partner())
 
     own_rows.wait()
     for o in (1, 2, 3):
-        r3[o].wait_recv()
+        r4[o].wait_recv()
 
     def split_rows(k, carry):
         top, rest = split(full[k].reshape(bands, full.shape[-1]))
@@ -592,11 +602,11 @@
     width = cells // RING // PARTS
     half = bands // 2
     sub = half // 2
-    rows = bands // (4 * RING)
+    rows = bands // (2 * RING * RING)
     strip = group * projs // RING
     f32, bf16 = jnp.float32, jnp.bfloat16
     counts = [
-        (PARTS, 3), (PARTS, 3), (3, 2), (3, 3, 2), (3,), (slots // GROUP,), (2, 2, 3), (2, 2, 3), (3,), (3,),
+        (PARTS, 3), (PARTS, 3), (3,), (3, 3, 2), (3, 3, 2), (3,), (slots // GROUP,), (2, 2, 3), (2, 2, 3), (3,), (3,),
         (2, 2, 3), (2, 2, RING), (2, RING), (2, 4 * RING),
     ]
     dma = pltpu.SemaphoreType.DMA
@@ -614,7 +624,7 @@
         scratch_shapes=[
             pltpu.VMEM((PARTS, RING, bands, width), f32),
             pltpu.VMEM((RING, bands, cells // RING), f32),
-            pltpu.VMEM((RING, 2, RING, 2, rows, all_bands), f32),
+            pltpu.VMEM((RING, RING, RING, 2, rows, all_bands), f32),
             pltpu.VMEM((bands, RING * all_bands), bf16),
             pltpu.VMEM((bands, RING * all_bands), bf16),
             pltpu.VMEM((cells // LANES, bands, LANES), bf16),
@@ -643,7 +653,7 @@
         ),
         name="exchange",
     )(
-        table, weights, orbitals, projectors, rotation.reshape(2, RING, 2, rows, all_bands), matrices
+        table, weights, orbitals, projectors, rotation.reshape(RING, RING, 2, rows, all_bands), matrices
     )
     return factors.reshape(atoms, bands, projs), rotated
 

time: 142 us -> 140 us (0.986)
  Pallas kernels: 142 us -> 140 us
    pallas_call x1, Pallas kernels: 16.7 us -> 14.1 us  [update(): pl.pallas_call(update_kernel, out_shape=jax.ShapeDtypeStruct((bands, cell...]
    pallas_call x1, Pallas kernels: 121 us -> 123 us  [exchange(): pl.pallas_call(exchange_kernel, out_shape=(jax.ShapeDtypeStruct((RING, RI...]
where the time goes in v4:
time: 140 us
  Pallas kernels  140 us (100%)
    pallas_call x1, Pallas kernels, exchange(): pl.pallas_call(exchange_kernel, out_shape=(jax.ShapeDtypeStruct((RING, RI...  123 us
    pallas_call x1, Pallas kernels, update(): pl.pallas_call(update_kernel, out_shape=jax.ShapeDtypeStruct((bands, cell...  14.1 us

profile of v4, /device:TPU:1, one launch (start us, length us, event | category | flops | bytes accessed | tf_op | source)
XLA Modules:
  0.0 139.9 jit_solution(4782930602945797156)
XLA Ops:
  0.0 2.3 %list_slots.1 = (s32[16,128]{1,0:T(8,128)}, f32[16,128]{1,0:T(8,128)}) custom-call(s32[1]{0:T(128)} %bitcast.dom, s32[32]{0:T(128)} %start.1, s32[32,32]{1,0:T(8,128)} %slot_atom.1, s32[96]{0:T(128)} %home.1), custom_call_target="tpu_custom_call" | custom-call | tf_op jit(solution)/shard_map/list_slots/pallas_call | solution.py:86
  2.3 123.3 %exchange.1 = (f32[4,4,2,3,256,128]{5,4,3,2,1,0:T(8,128)}, f32[256,4096]{1,0:T(8,128)}) custom-call(s32[16,128]{1,0:T(8,128)} %get-tuple-element.9.table, f32[16,128]{1,0:T(8,128)} %get-tuple-element.10.weights, f32[256,4096]{1,0:T(8,128)} %orbitals.1, f32[32,512,128]{2,1,0:T(8,128)} %refs_8_.1, f32[4,4,2,8,1024]{4,3,2,1,0:T(8,128)} %bitcast.11, ...), custom_call_target="tpu_custom_call" | custom-call | tf_op jit(solution)/shard_map/exchange/pallas_call | solution.py:614
  125.6 14.1 %update.1 = f32[256,4096]{1,0:T(8,128)} custom-call(s32[16,128]{1,0:T(8,128)} %get-tuple-element.9.table, f32[96,256,128]{2,1,0:T(8,128)} %bitcast.3, f32[96,256,128]{2,1,0:T(8,128)} %bitcast.4, f32[96,256,128]{2,1,0:T(8,128)} %bitcast.5, f32[96,256,128]{2,1,0:T(8,128)} %bitcast.6, f32[96,256,128]{2,1,0:T(8,128)} %bitcast.7, f32[96,256,128]{2,1,0:T(8,128)} %bitcast.8, ...), custom_call_target="tpu_custom_call" | custom-call | flops 3221225472 | bytes 20971520 | tf_op jit(solution)/shard_map/update/pallas_call | solution.py:141

commit v5 on v4

--- a/solution.py
+++ b/solution.py
@@ -96,31 +96,26 @@
 def update_kernel(table, *refs):
     group = UPDATE_GROUP
     factors = refs[:group]
-    projectors, rotated, out = refs[group : group + 3]
-    pads, base = refs[group + 3 : -2], refs[-2]
+    columns, rotated, out, base, sem = refs[group:]
     step = pl.program_id(0)
-    fetch = pltpu.make_async_copy(rotated, base, refs[-1])
-    _, window, _ = projectors.shape
-    cells = out.shape[1]
-    wide = window + LANES
+    _, both, wide = columns.shape
+    projs = both // 2
+    fetch = pltpu.make_async_copy(rotated, base, sem)
 
     @pl.when(step == 0)
     def _():
         fetch.start()
-        for pad in pads:
-            clear(pad, window)
         out[...] = jnp.zeros_like(out)
 
     for k in range(group):
         slot = step * group + k
-        cell, shift = pl.multiple_of(table[TILE, slot] * LANES, LANES), table[SHIFT, slot]
-        p_high, p_low = shifted(projectors[k], pads[k], shift, window, wide)
+        cell = pl.multiple_of(table[TILE, slot] * LANES, LANES)
         f_high, f_low = split(factors[k][0])
-        update = dot_nt(
+        p_high, p_low = columns[k, :projs, :], columns[k, projs:, :]
+        out[:, pl.ds(cell, wide)] += dot(
             jnp.concatenate([f_high, f_low, f_high], axis=1),
-            jnp.concatenate([p_high, p_high, p_low], axis=1),
+            jnp.concatenate([p_high, p_high, p_low], axis=0),
         )
-        out[:, pl.ds(cell, wide)] += update
 
     @pl.when(step == pl.num_programs(0) - 1)
     def _():
@@ -128,9 +123,10 @@
         out[...] += base[...]
 
 
-def update(table, factors, projectors, rotated):
-    slots, window, projs = projectors.shape
+def update(table, factors, columns, rotated):
+    slots, both, wide = columns.shape
     bands, cells = rotated.shape
+    projs = both // 2
 
     def factor_spec(k):
         return pl.BlockSpec(
@@ -146,21 +142,20 @@
             grid=(slots // UPDATE_GROUP,),
             in_specs=[factor_spec(k) for k in range(UPDATE_GROUP)]
             + [
-                pl.BlockSpec((UPDATE_GROUP, window, projs), lambda i, *_: (i, 0, 0)),
+                pl.BlockSpec((UPDATE_GROUP, both, wide), lambda i, *_: (i, 0, 0)),
                 pl.BlockSpec(memory_space=pltpu.MemorySpace.HBM),
             ],
             out_specs=pl.BlockSpec(
                 (bands, cells), lambda i, *_: (0, 0), pipeline_mode=pl.Buffered(1)
             ),
-            scratch_shapes=[pltpu.VMEM((window + 2 * LANES, projs), jnp.float32)] * UPDATE_GROUP
-            + [pltpu.VMEM((bands, cells), jnp.float32), pltpu.SemaphoreType.DMA],
+            scratch_shapes=[pltpu.VMEM((bands, cells), jnp.float32), pltpu.SemaphoreType.DMA],
         ),
         cost_estimate=pl.CostEstimate(
-            flops=6 * slots * window * bands * projs, bytes_accessed=20 << 20, transcendentals=0
+            flops=6 * slots * wide * bands * projs, bytes_accessed=22 << 20, transcendentals=0
         ),
         compiler_params=pltpu.CompilerParams(vmem_limit_bytes=60 << 20),
         name="update",
-    )(table, *([factors] * UPDATE_GROUP), projectors, rotated)
+    )(table, *([factors] * UPDATE_GROUP), columns, rotated)
 
 
 MESH = pl.DeviceIdType.MESH
@@ -201,10 +196,10 @@
 
 
 def exchange_kernel(
-    table, weights, orbitals, projectors, rotation, matrices, factors, rotated,
+    table, weights, orbitals, projectors, rotation, matrices, factors, rotated, columns,
     cells_in, cells_out, full, high_rows, low_rows, high_cells, low_cells, tiles, windows, mate, total, hop1, hop2, hop3, hop4,
-    turn, turn_in, turn_out, turned, owned, pads,
-    sem_load, sem_keep, sem_own, *sems
+    turn, turn_in, turn_out, turned, owned, pads, ready,
+    sem_load, sem_keep, sem_own, sem_ready, *sems
 ):
     link = Links()
     b, x, z, c = link.band, link.x, link.z, link.core
@@ -254,23 +249,28 @@
             return factors.at[t, u, core, :, rows, :]
         return factors.at[u, t, core, :, rows, :]
 
+    r1 = {}
+    for o in (1, 2, 3):
+        r1[o] = push(rotation.at[x, z, c], full.at[b, x, z, c], "r1", (o - 1,), link.at_band(o))
+    yin, own_cells = {}, []
+
+    def send_cells(i):
+        for o in (1, 2, 3):
+            src = orbitals.at[:, tile_of(ring(b, o) * parts + i, width)]
+            yin[i, o] = push(src, cells_in.at[i, b], "yin", (i, o - 1), link.at_band(o))
+
+    send_cells(0)
     stage = [keep(orbitals.at[:, tile_of(q, quarter)], cells_out.at[q], sem_load.at[q]) for q in range(RING)]
     eighth = slots // RING
     stage_tiles = [
         keep(projectors.at[pl.ds(q * eighth, eighth)], tiles.at[pl.ds(q * eighth, eighth)], sem_load.at[RING + q])
         for q in range(RING)
     ]
-    r1 = {}
-    for o in (1, 2, 3):
-        r1[o] = push(rotation.at[x, z, c], full.at[b, x, z, c], "r1", (o - 1,), link.at_band(o))
     own_rows = keep(rotation, full.at[b], sem_own.at[0])
-    yin, own_cells = {}, []
+    for i in range(1, parts):
+        send_cells(i)
     for i in range(parts):
-        for o in (1, 2, 3):
-            src = orbitals.at[:, tile_of(ring(b, o) * parts + i, width)]
-            yin[i, o] = push(src, cells_in.at[i, b], "yin", (i, o - 1), link.at_band(o))
         own_cells.append(keep(orbitals.at[:, tile_of(b * parts + i, width)], cells_in.at[i, b], sem_keep.at[i]))
-
     for k in range(GROUP):
         clear(pads.at[k], window)
     r2, r3, r4 = {}, {}, {}
@@ -417,16 +417,18 @@
             return carry
 
         lax.fori_loop(0, RING, body, 0)
-    def give(i):
+    def give(i, offsets=(1, 2, 3)):
         columns = tile_of(b * parts + i, width)
-        for o in (1, 2, 3):
+        for o in offsets:
             src = cells_out.at[ring(b, o), :, pl.ds(i * width, width)]
             yout[i, o] = push(src, rotated.at[:, columns], "yout", (i, o - 1), link.at_band(o))
-        own_out.append(keep(cells_out.at[b, :, pl.ds(i * width, width)], rotated.at[:, columns], sem_keep.at[parts + i]))
+        if 2 in offsets:
+            own_out.append(
+                keep(cells_out.at[b, :, pl.ds(i * width, width)], rotated.at[:, columns], sem_keep.at[parts + i])
+            )
 
     for i in range(parts // 2):
         rotate(i)
-    give(0)
 
     for h in range(2):
         t = first[h]
@@ -485,7 +487,7 @@
     for o in (1, 2, 3):
         swap[o] = push(turn.at[strip_at(ring(b, o))], turn_in.at[b], "sum", (o - 1,), link.at_band(o))
     turn_in[b] = turn[strip_at(b), :]
-    give(1)
+    give(0, (1, 3))
 
     for o in (1, 2, 3):
         swap[o].wait_recv()
@@ -503,7 +505,8 @@
         back[o] = push(turn_out.at[ring(b, o)], turned.at[strip_at(b)], "back", (o - 1,), link.at_band(o))
     turned[strip_at(b), :] = turn_out[b]
 
-    for i in range(2, parts // 2 + 2):
+    give(0, (2,))
+    for i in range(1, parts // 2 + 2):
         give(i)
     for i in range(parts // 2 + 2, parts):
         rotate(i)
@@ -523,6 +526,31 @@
     def to_core(src, h, t, u, index):
         mate_core.append(push(src, factor_at(h, t, u, c), "core", (h, index), link.partner()))
 
+    pairs = ready.shape[0]
+
+    def put(slot, index):
+        return pltpu.make_async_copy(ready.at[slot], columns.at[index], sem_ready.at[slot])
+
+    def prepare(low, high):
+        def body(step, carry):
+            for k in range(pairs):
+                index = step * pairs + k
+
+                @pl.when(step > 0)
+                def _(k=k, index=index):
+                    put(k, index).wait()
+
+                pad = pads.at[k]
+                pad[pl.ds(LANES, window), :] = tiles[index]
+                high, low = split(pad[pl.ds(LANES - table[SHIFT, index], wide), :].T)
+                ready[k, pl.ds(0, projs), :] = high
+                ready[k, pl.ds(projs, projs), :] = low
+                put(k, index).start()
+            return carry
+
+        lax.fori_loop(low, high, body, 0)
+
+    share = slots // pairs // 8
     ag1, ag2, agf = {}, {}, {}
     for h in range(2):
         t, s = first[h], second[h]
@@ -541,24 +569,28 @@
     lines = (0, 3, 1, 2)
     for h in range(2):
         spread(h, 0, owned.at[:, pl.ds(h * half, half)], second[h])
+    prepare(0, share)
     for h in range(2):
         t, s = first[h], second[h]
         for d, back, peer in ((0, 3, 1), (1, 1, 3)):
             ag1[h, d, 0].wait_recv()
             piece = factor_at(h, t, ring(s, back), c, d * sub, sub)
             ag1[h, d, 2] = push(piece, piece, "ag1", (h, d, 2), at_second[h](peer))
+    prepare(share, 2 * share)
     for h in range(2):
         t, s = first[h], second[h]
         for d, r in ((0, 1), (1, 2)):
             ag1[h, d, 1].wait_recv()
             u = ring(s, lines[r])
             spread(h, r, factor_at(h, t, u, c), u)
+    prepare(2 * share, 3 * share)
     for h in range(2):
         t, s = first[h], second[h]
         ag1[h, 0, 2].wait_recv()
         ag1[h, 1, 2].wait_recv()
         u = ring(s, 2)
         spread(h, 3, factor_at(h, t, u, c), u)
+    prepare(3 * share, 4 * share)
 
     for r in range(RING):
         for h in range(2):
@@ -570,6 +602,7 @@
                 if (r < 2) == (d == 0):
                     agf[h, r] = push(piece, piece, "agf", (h, r), at_first[h](peer))
                 to_core(piece, h, t, u, RING * (1 + d) + r)
+        prepare((4 + r) * share, (5 + r) * share)
     for r in range(RING):
         for h in range(2):
             u = ring(second[h], lines[r])
@@ -584,6 +617,8 @@
     for copy in own_out:
         copy.wait()
     own_factor.wait()
+    for k in range(pairs):
+        put(k, k).wait()
     for copy in started:
         copy.wait_send()
     for step in range(slots // GROUP):
@@ -611,16 +646,17 @@
     ]
     dma = pltpu.SemaphoreType.DMA
     in_hbm = pl.BlockSpec(memory_space=pltpu.MemorySpace.HBM)
-    factors, rotated = pl.pallas_call(
+    factors, rotated, columns = pl.pallas_call(
         exchange_kernel,
         out_shape=(
             jax.ShapeDtypeStruct((RING, RING, 2, group, bands, projs), f32),
             jax.ShapeDtypeStruct((bands, cells), f32),
+            jax.ShapeDtypeStruct((slots, 2 * projs, window + LANES), bf16),
         ),
         in_specs=[pl.BlockSpec(memory_space=pltpu.SMEM)] * 2
         + [in_hbm] * 3
         + [pl.BlockSpec(memory_space=pltpu.VMEM)],
-        out_specs=[in_hbm] * 2,
+        out_specs=[in_hbm] * 3,
         scratch_shapes=[
             pltpu.VMEM((PARTS, RING, bands, width), f32),
             pltpu.VMEM((RING, bands, cells // RING), f32),
@@ -643,8 +679,10 @@
             pltpu.VMEM((group * projs, bands), f32),
             pltpu.VMEM((group, bands, projs), f32),
             pltpu.VMEM((GROUP, window + 2 * LANES, projs), f32),
+            pltpu.VMEM((2, 2 * projs, window + LANES), bf16),
             dma((2 * RING,)),
             dma((2 * PARTS,)),
+            dma((2,)),
             dma((2,)),
         ]
         + [dma(shape) for shape in counts for _ in range(2)],
@@ -655,7 +693,7 @@
     )(
         table, weights, orbitals, projectors, rotation.reshape(RING, RING, 2, rows, all_bands), matrices
     )
-    return factors.reshape(atoms, bands, projs), rotated
+    return factors.reshape(atoms, bands, projs), rotated, columns
 
 
 def per_device(orbitals, projectors, window_start, slot_atom, atom_home, atom_matrices, rotation):
@@ -664,8 +702,8 @@
     table, weights = list_slots(
         dom, window_start, slot_atom, atom_home, atom_matrices.shape[0], orbitals.shape[1], window + LANES
     )
-    factors, rotated = exchange(table, weights, orbitals, projectors, rotation, atom_matrices)
-    return update(table, factors, projectors, rotated)
+    factors, rotated, columns = exchange(table, weights, orbitals, projectors, rotation, atom_matrices)
+    return update(table, factors, columns, rotated)
 
 
 def solution(mesh):

time: 140 us -> 141 us (level)
    pallas_call x1, Pallas kernels: 123 us -> 125 us  [exchange(): pl.pallas_call(exchange_kernel, out_shape=(jax.ShapeDtypeStruct((RING, RI...]
where the time goes in v5:
time: 141 us
  Pallas kernels  141 us (100%)
    pallas_call x1, Pallas kernels, exchange(): pl.pallas_call(exchange_kernel, out_shape=(jax.ShapeDtypeStruct((RING, RI...  125 us
    pallas_call x1, Pallas kernels, update(): pl.pallas_call(update_kernel, out_shape=jax.ShapeDtypeStruct((bands, cell...  13.2 us

profile of v5, /device:TPU:1, one launch (start us, length us, event | category | flops | bytes accessed | tf_op | source)
XLA Modules:
  0.0 140.7 jit_solution(6235127943359894437)
XLA Ops:
  0.0 2.3 %list_slots.1 = (s32[16,128]{1,0:T(8,128)}, f32[16,128]{1,0:T(8,128)}) custom-call(s32[1]{0:T(128)} %bitcast.dom, s32[32]{0:T(128)} %start.1, s32[32,32]{1,0:T(8,128)} %slot_atom.1, s32[96]{0:T(128)} %home.1), custom_call_target="tpu_custom_call" | custom-call | tf_op jit(solution)/shard_map/list_slots/pallas_call | solution.py:86
  2.3 125.1 %exchange.1 = (f32[4,4,2,3,256,128]{5,4,3,2,1,0:T(8,128)}, f32[256,4096]{1,0:T(8,128)}, bf16[32,256,640]{2,1,0:T(8,128)(2,1)}) custom-call(s32[16,128]{1,0:T(8,128)} %get-tuple-element.10.table, f32[16,128]{1,0:T(8,128)} %get-tuple-element.11.weights, f32[256,4096]{1,0:T(8,128)} %orbitals.1, f32[32,512,128]{2,1,0:T(8,128)} %projectors.1, ...), custom_call_target="tpu_custom_call" | custom-call | tf_op jit(solution)/shard_map/exchange/pallas_call | solution.py:649
  127.4 13.2 %update.1 = f32[256,4096]{1,0:T(8,128)} custom-call(s32[16,128]{1,0:T(8,128)} %get-tuple-element.10.table, f32[96,256,128]{2,1,0:T(8,128)} %bitcast.3, f32[96,256,128]{2,1,0:T(8,128)} %bitcast.4, f32[96,256,128]{2,1,0:T(8,128)} %bitcast.5, f32[96,256,128]{2,1,0:T(8,128)} %bitcast.6, f32[96,256,128]{2,1,0:T(8,128)} %bitcast.7, f32[96,256,128]{2,1,0:T(8,128)} %bitcast.8, ...), custom_call_target="tpu_custom_call" | custom-call | flops 4026531840 | bytes 23068672 | tf_op jit(solution)/shard_map/update/pallas_call | solution.py:137

commit v6 on v5

--- a/solution.py
+++ b/solution.py
@@ -236,30 +236,6 @@
     peers = [f(o) for f in (link.at_band, link.at_x, link.at_z) for o in (1, 2, 3)] + [link.partner()]
     for peer in peers:
         pl.semaphore_signal(barrier, inc=1, device_id=peer, device_id_type=MESH)
-    pl.semaphore_wait(barrier, len(peers))
-
-    first = (x, z)
-    second = (z, x)
-    at_first = (link.at_x, link.at_z)
-    at_second = (link.at_z, link.at_x)
-
-    def factor_at(h, t, u, core, low=0, size=None):
-        rows = pl.ds(h * half + low, half if size is None else size)
-        if h == 0:
-            return factors.at[t, u, core, :, rows, :]
-        return factors.at[u, t, core, :, rows, :]
-
-    r1 = {}
-    for o in (1, 2, 3):
-        r1[o] = push(rotation.at[x, z, c], full.at[b, x, z, c], "r1", (o - 1,), link.at_band(o))
-    yin, own_cells = {}, []
-
-    def send_cells(i):
-        for o in (1, 2, 3):
-            src = orbitals.at[:, tile_of(ring(b, o) * parts + i, width)]
-            yin[i, o] = push(src, cells_in.at[i, b], "yin", (i, o - 1), link.at_band(o))
-
-    send_cells(0)
     stage = [keep(orbitals.at[:, tile_of(q, quarter)], cells_out.at[q], sem_load.at[q]) for q in range(RING)]
     eighth = slots // RING
     stage_tiles = [
@@ -267,38 +243,45 @@
         for q in range(RING)
     ]
     own_rows = keep(rotation, full.at[b], sem_own.at[0])
+    for k in range(GROUP):
+        clear(pads.at[k], window)
+    pl.semaphore_wait(barrier, len(peers))
+
+    first = (x, z)
+    second = (z, x)
+    at_first = (link.at_x, link.at_z)
+    at_second = (link.at_z, link.at_x)
+
+    def factor_at(h, t, u, core, low=0, size=None):
+        rows = pl.ds(h * half + low, half if size is None else size)
+        if h == 0:
+            return factors.at[t, u, core, :, rows, :]
+        return factors.at[u, t, core, :, rows, :]
+
+    r1 = {}
+    for o in (1, 2, 3):
+        r1[o] = push(rotation.at[x, z, c], full.at[b, x, z, c], "r1", (o - 1,), link.at_band(o))
+    yin, own_cells = {}, []
+
+    def send_cells(i):
+        for o in (1, 2, 3):
+            src = orbitals.at[:, tile_of(ring(b, o) * parts + i, width)]
+            yin[i, o] = push(src, cells_in.at[i, b], "yin", (i, o - 1), link.at_band(o))
+
+    send_cells(0)
     for i in range(1, parts):
         send_cells(i)
     for i in range(parts):
         own_cells.append(keep(orbitals.at[:, tile_of(b * parts + i, width)], cells_in.at[i, b], sem_keep.at[i]))
-    for k in range(GROUP):
-        clear(pads.at[k], window)
     r2, r3, r4 = {}, {}, {}
     columns_of = [pl.ds(h * (full.shape[-1] // 2), full.shape[-1] // 2) for h in range(2)]
-    for o in (1, 2, 3):
-        r1[o].wait_recv()
-        for h in range(2):
-            piece = full.at[ring(b, RING - o), x, z, c, :, columns_of[h]]
-            for p in (1, 2, 3):
-                r2[o, p, h] = push(piece, piece, "r2", (o - 1, p - 1, h), at_first[h](p))
+    routes = [(1, 0, slice(None)), (2, 0, columns_of[0]), (2, 1, columns_of[1]), (3, 1, slice(None))]
     for q in range(RING):
         stage[q].wait()
         top, rest = split(cells_out[q])
         for m in range(quarter // LANES):
             high_cells[q * (quarter // LANES) + m] = top[:, m * LANES : (m + 1) * LANES]
             low_cells[q * (quarter // LANES) + m] = rest[:, m * LANES : (m + 1) * LANES]
-    for o in (1, 2, 3):
-        k = ring(b, RING - o)
-        for h in range(2):
-            for p in (1, 2, 3):
-                r2[o, p, h].wait_recv()
-            if h == 0:
-                piece = full.at[k, :, z, c, :, columns_of[h]]
-            else:
-                piece = full.at[k, x, :, c, :, columns_of[h]]
-            for p in (1, 2, 3):
-                r3[o, p, h] = push(piece, piece, "r3", (o - 1, p - 1, h), at_second[h](p))
-
     def to_mate(step):
         group_at = pl.ds(step * GROUP, GROUP)
         return pltpu.make_async_remote_copy(
@@ -350,6 +333,21 @@
     for q in range(RING):
         stage_tiles[q].wait()
         lax.fori_loop(q * steps // RING, (q + 1) * steps // RING, take, 0)
+        if q == 0:
+            for o in (1, 2, 3):
+                r1[o].wait_recv()
+            for n, (o, h, span) in enumerate(routes):
+                piece = full.at[ring(b, RING - o), x, z, c, :, span]
+                for p in (1, 2, 3):
+                    r2[n, p] = push(piece, piece, "r2", (n, p - 1), at_first[h](p))
+        if q == 2:
+            for n, (o, h, span) in enumerate(routes):
+                k = ring(b, RING - o)
+                for p in (1, 2, 3):
+                    r2[n, p].wait_recv()
+                piece = full.at[k, :, z, c, :, span] if h == 0 else full.at[k, x, :, c, :, span]
+                for p in (1, 2, 3):
+                    r3[n, p] = push(piece, piece, "r3", (n, p - 1), at_second[h](p))
     for step in range(steps):
         to_mate(step).wait_recv()
     for h in range(2):
@@ -380,10 +378,9 @@
         add_rows(h, t, 2, hop1)
         one[h, 1, 2] = push(total.at[h, t, high2], hop2.at[h, 1, high2], "one", (h, 1, 2), at_first[h](3))
 
+    for copy in r3.values():
+        copy.wait_recv()
     for o in (1, 2, 3):
-        for h in range(2):
-            for p in (1, 2, 3):
-                r3[o, p, h].wait_recv()
         mine = full.at[ring(b, RING - o), :, :, c]
         r4[o] = push(mine, mine, "r4", (o - 1,), link.partner())
 
@@ -417,18 +414,19 @@
             return carry
 
         lax.fori_loop(0, RING, body, 0)
-    def give(i, offsets=(1, 2, 3)):
-        columns = tile_of(b * parts + i, width)
+    def give(unit, offsets=(1, 2, 3)):
+        i, lower = unit // 2, unit % 2
+        rows, columns = pl.ds(lower * half, half), tile_of(b * parts + i, width)
         for o in offsets:
-            src = cells_out.at[ring(b, o), :, pl.ds(i * width, width)]
-            yout[i, o] = push(src, rotated.at[:, columns], "yout", (i, o - 1), link.at_band(o))
+            src = cells_out.at[ring(b, o), rows, pl.ds(i * width, width)]
+            yout[unit, o] = push(src, rotated.at[rows, columns], "yout", (unit, o - 1), link.at_band(o))
         if 2 in offsets:
-            own_out.append(
-                keep(cells_out.at[b, :, pl.ds(i * width, width)], rotated.at[:, columns], sem_keep.at[parts + i])
-            )
-
-    for i in range(parts // 2):
-        rotate(i)
+            src = cells_out.at[b, rows, pl.ds(i * width, width)]
+            own_out.append(keep(src, rotated.at[rows, columns], sem_keep.at[parts + unit]))
+
+    rotate(0)
+    rotate(1)
+    give(0)
 
     for h in range(2):
         t = first[h]
@@ -468,8 +466,7 @@
             total.at[h, t, prv, :, upper], hop4.at[h, 1, :, upper], "two", (h, 1, 2), at_second[h](3)
         )
 
-    rotate(parts // 2)
-    rotate(parts // 2 + 1)
+    rotate(2)
 
     for h in range(2):
         t, s = first[h], second[h]
@@ -487,7 +484,7 @@
     for o in (1, 2, 3):
         swap[o] = push(turn.at[strip_at(ring(b, o))], turn_in.at[b], "sum", (o - 1,), link.at_band(o))
     turn_in[b] = turn[strip_at(b), :]
-    give(0, (1, 3))
+    give(1, (1, 3))
 
     for o in (1, 2, 3):
         swap[o].wait_recv()
@@ -505,12 +502,12 @@
         back[o] = push(turn_out.at[ring(b, o)], turned.at[strip_at(b)], "back", (o - 1,), link.at_band(o))
     turned[strip_at(b), :] = turn_out[b]
 
-    give(0, (2,))
-    for i in range(1, parts // 2 + 2):
-        give(i)
-    for i in range(parts // 2 + 2, parts):
-        rotate(i)
-        give(i)
+    give(1, (2,))
+    for unit in range(2, 6):
+        give(unit)
+    rotate(3)
+    give(6)
+    give(7)
 
     for o in (1, 2, 3):
         back[o].wait_recv()
@@ -625,7 +622,7 @@
         to_mate(step).wait_send()
 
 
-PARTS = 8
+PARTS = 4
 
 
 def exchange(table, weights, orbitals, projectors, rotation, matrices):
@@ -641,7 +638,7 @@
     strip = group * projs // RING
     f32, bf16 = jnp.float32, jnp.bfloat16
     counts = [
-        (PARTS, 3), (PARTS, 3), (3,), (3, 3, 2), (3, 3, 2), (3,), (slots // GROUP,), (2, 2, 3), (2, 2, 3), (3,), (3,),
+        (PARTS, 3), (2 * PARTS, 3), (3,), (4, 3), (4, 3), (3,), (slots // GROUP,), (2, 2, 3), (2, 2, 3), (3,), (3,),
         (2, 2, 3), (2, 2, RING), (2, RING), (2, 4 * RING),
     ]
     dma = pltpu.SemaphoreType.DMA
@@ -681,7 +678,7 @@
             pltpu.VMEM((GROUP, window + 2 * LANES, projs), f32),
             pltpu.VMEM((2, 2 * projs, window + LANES), bf16),
             dma((2 * RING,)),
-            dma((2 * PARTS,)),
+            dma((3 * PARTS,)),
             dma((2,)),
             dma((2,)),
         ]

time: 141 us -> 134 us (0.950)
  Pallas kernels: 141 us -> 133 us
    pallas_call x1, Pallas kernels: 125 us -> 118 us  [exchange(): pl.pallas_call(exchange_kernel, out_shape=(jax.ShapeDtypeStruct((RING, RI...]
where the time goes in v6:
time: 134 us
  Pallas kernels  133 us (99%)
    pallas_call x1, Pallas kernels, exchange(): pl.pallas_call(exchange_kernel, out_shape=(jax.ShapeDtypeStruct((RING, RI...  118 us
    pallas_call x1, Pallas kernels, update(): pl.pallas_call(update_kernel, out_shape=jax.ShapeDtypeStruct((bands, cell...  13.2 us

profile of v6, /device:TPU:1, one launch (start us, length us, event | category | flops | bytes accessed | tf_op | source)
XLA Modules:
  0.0 133.7 jit_solution(17658801713070230152)
XLA Ops:
  0.0 2.3 %list_slots.1 = (s32[16,128]{1,0:T(8,128)}, f32[16,128]{1,0:T(8,128)}) custom-call(s32[1]{0:T(128)} %bitcast.dom, s32[32]{0:T(128)} %start.1, s32[32,32]{1,0:T(8,128)} %slot_atom.1, s32[96]{0:T(128)} %home.1), custom_call_target="tpu_custom_call" | custom-call | tf_op jit(solution)/shard_map/list_slots/pallas_call | solution.py:86
  2.3 118.0 %exchange.1 = (f32[4,4,2,3,256,128]{5,4,3,2,1,0:T(8,128)}, f32[256,4096]{1,0:T(8,128)}, bf16[32,256,640]{2,1,0:T(8,128)(2,1)}) custom-call(s32[16,128]{1,0:T(8,128)} %get-tuple-element.10.table, f32[16,128]{1,0:T(8,128)} %get-tuple-element.11.weights, f32[256,4096]{1,0:T(8,128)} %orbitals.1, f32[32,512,128]{2,1,0:T(8,128)} %projectors.1, ...), custom_call_target="tpu_custom_call" | custom-call | tf_op jit(solution)/shard_map/exchange/pallas_call | solution.py:646
  120.3 13.2 %update.1 = f32[256,4096]{1,0:T(8,128)} custom-call(s32[16,128]{1,0:T(8,128)} %get-tuple-element.10.table, f32[96,256,128]{2,1,0:T(8,128)} %bitcast.3, f32[96,256,128]{2,1,0:T(8,128)} %bitcast.4, f32[96,256,128]{2,1,0:T(8,128)} %bitcast.5, f32[96,256,128]{2,1,0:T(8,128)} %bitcast.6, f32[96,256,128]{2,1,0:T(8,128)} %bitcast.7, f32[96,256,128]{2,1,0:T(8,128)} %bitcast.8, ...), custom_call_target="tpu_custom_call" | custom-call | flops 4026531840 | bytes 23068672 | tf_op jit(solution)/shard_map/update/pallas_call | solution.py:137

commit v7 on v6

--- a/solution.py
+++ b/solution.py
@@ -333,14 +333,14 @@
     for q in range(RING):
         stage_tiles[q].wait()
         lax.fori_loop(q * steps // RING, (q + 1) * steps // RING, take, 0)
-        if q == 0:
+        if q == 1:
             for o in (1, 2, 3):
                 r1[o].wait_recv()
             for n, (o, h, span) in enumerate(routes):
                 piece = full.at[ring(b, RING - o), x, z, c, :, span]
                 for p in (1, 2, 3):
                     r2[n, p] = push(piece, piece, "r2", (n, p - 1), at_first[h](p))
-        if q == 2:
+        if q == 3:
             for n, (o, h, span) in enumerate(routes):
                 k = ring(b, RING - o)
                 for p in (1, 2, 3):

time: 134 us -> 131 us (0.978)
  Pallas kernels: 133 us -> 130 us
    pallas_call x1, Pallas kernels: 118 us -> 115 us  [exchange(): pl.pallas_call(exchange_kernel, out_shape=(jax.ShapeDtypeStruct((RING, RI...]
where the time goes in v7:
time: 131 us
  Pallas kernels  130 us (99%)
    pallas_call x1, Pallas kernels, exchange(): pl.pallas_call(exchange_kernel, out_shape=(jax.ShapeDtypeStruct((RING, RI...  115 us
    pallas_call x1, Pallas kernels, update(): pl.pallas_call(update_kernel, out_shape=jax.ShapeDtypeStruct((bands, cell...  13.2 us

profile of v7, /device:TPU:1, one launch (start us, length us, event | category | flops | bytes accessed | tf_op | source)
XLA Modules:
  0.0 130.6 jit_solution(12863431297067143266)
XLA Ops:
  0.0 2.3 %list_slots.1 = (s32[16,128]{1,0:T(8,128)}, f32[16,128]{1,0:T(8,128)}) custom-call(s32[1]{0:T(128)} %bitcast.dom, s32[32]{0:T(128)} %start.1, s32[32,32]{1,0:T(8,128)} %slot_atom.1, s32[96]{0:T(128)} %home.1), custom_call_target="tpu_custom_call" | custom-call | tf_op jit(solution)/shard_map/list_slots/pallas_call | solution.py:86
  2.3 114.9 %exchange.1 = (f32[4,4,2,3,256,128]{5,4,3,2,1,0:T(8,128)}, f32[256,4096]{1,0:T(8,128)}, bf16[32,256,640]{2,1,0:T(8,128)(2,1)}) custom-call(s32[16,128]{1,0:T(8,128)} %get-tuple-element.10.table, f32[16,128]{1,0:T(8,128)} %get-tuple-element.11.weights, f32[256,4096]{1,0:T(8,128)} %orbitals.1, f32[32,512,128]{2,1,0:T(8,128)} %projectors.1, ...), custom_call_target="tpu_custom_call" | custom-call | tf_op jit(solution)/shard_map/exchange/pallas_call | solution.py:646
  117.2 13.2 %update.1 = f32[256,4096]{1,0:T(8,128)} custom-call(s32[16,128]{1,0:T(8,128)} %get-tuple-element.10.table, f32[96,256,128]{2,1,0:T(8,128)} %bitcast.3, f32[96,256,128]{2,1,0:T(8,128)} %bitcast.4, f32[96,256,128]{2,1,0:T(8,128)} %bitcast.5, f32[96,256,128]{2,1,0:T(8,128)} %bitcast.6, f32[96,256,128]{2,1,0:T(8,128)} %bitcast.7, f32[96,256,128]{2,1,0:T(8,128)} %bitcast.8, ...), custom_call_target="tpu_custom_call" | custom-call | flops 4026531840 | bytes 23068672 | tf_op jit(solution)/shard_map/update/pallas_call | solution.py:137

commit v8 on v7

--- a/solution.py
+++ b/solution.py
@@ -269,8 +269,7 @@
             yin[i, o] = push(src, cells_in.at[i, b], "yin", (i, o - 1), link.at_band(o))
 
     send_cells(0)
-    for i in range(1, parts):
-        send_cells(i)
+    send_cells(1)
     for i in range(parts):
         own_cells.append(keep(orbitals.at[:, tile_of(b * parts + i, width)], cells_in.at[i, b], sem_keep.at[i]))
     r2, r3, r4 = {}, {}, {}
@@ -333,6 +332,8 @@
     for q in range(RING):
         stage_tiles[q].wait()
         lax.fori_loop(q * steps // RING, (q + 1) * steps // RING, take, 0)
+        if q < 2:
+            send_cells(2 + q)
         if q == 1:
             for o in (1, 2, 3):
                 r1[o].wait_recv()

time: 131 us -> 131 us (level)
  no operation moved by 1% of the time
where the time goes in v8:
time: 131 us; the launch traced here: 130 us
  Pallas kernels  130 us (99%)
    pallas_call x1, Pallas kernels, exchange(): pl.pallas_call(exchange_kernel, out_shape=(jax.ShapeDtypeStruct((RING, RI...  115 us
    pallas_call x1, Pallas kernels, update(): pl.pallas_call(update_kernel, out_shape=jax.ShapeDtypeStruct((bands, cell...  13.2 us

profile of v8, /device:TPU:1, one launch (start us, length us, event | category | flops | bytes accessed | tf_op | source)
XLA Modules:
  0.0 130.4 jit_solution(2478174779395773658)
XLA Ops:
  0.0 2.3 %list_slots.1 = (s32[16,128]{1,0:T(8,128)}, f32[16,128]{1,0:T(8,128)}) custom-call(s32[1]{0:T(128)} %bitcast.dom, s32[32]{0:T(128)} %start.1, s32[32,32]{1,0:T(8,128)} %slot_atom.1, s32[96]{0:T(128)} %home.1), custom_call_target="tpu_custom_call" | custom-call | tf_op jit(solution)/shard_map/list_slots/pallas_call | solution.py:86
  2.3 114.7 %exchange.1 = (f32[4,4,2,3,256,128]{5,4,3,2,1,0:T(8,128)}, f32[256,4096]{1,0:T(8,128)}, bf16[32,256,640]{2,1,0:T(8,128)(2,1)}) custom-call(s32[16,128]{1,0:T(8,128)} %get-tuple-element.10.table, f32[16,128]{1,0:T(8,128)} %get-tuple-element.11.weights, f32[256,4096]{1,0:T(8,128)} %orbitals.1, f32[32,512,128]{2,1,0:T(8,128)} %projectors.1, ...), custom_call_target="tpu_custom_call" | custom-call | tf_op jit(solution)/shard_map/exchange/pallas_call | solution.py:647
  117.1 13.2 %update.1 = f32[256,4096]{1,0:T(8,128)} custom-call(s32[16,128]{1,0:T(8,128)} %get-tuple-element.10.table, f32[96,256,128]{2,1,0:T(8,128)} %bitcast.3, f32[96,256,128]{2,1,0:T(8,128)} %bitcast.4, f32[96,256,128]{2,1,0:T(8,128)} %bitcast.5, f32[96,256,128]{2,1,0:T(8,128)} %bitcast.6, f32[96,256,128]{2,1,0:T(8,128)} %bitcast.7, f32[96,256,128]{2,1,0:T(8,128)} %bitcast.8, ...), custom_call_target="tpu_custom_call" | custom-call | flops 4026531840 | bytes 23068672 | tf_op jit(solution)/shard_map/update/pallas_call | solution.py:137
